TPU v7x, 256 devices: a whole 4x4x8 slice. The times are simulated.
256 devices in a mesh: row: 16 (over z, core), rep: 16 (over x, y).
Axes of the slice: x: 4, y: 4, z: 8, core: 2. Of those that a mesh axis runs over, the one named last changes fastest.
Arguments:
- basis: bfloat16 [32, 524288], P(None, ('row', 'rep')), may hold values from -6 to 6
- precond: float32 [524288], P(('row', 'rep')), may hold values from 0.1 to 0.4
- tiles: bfloat16 [8192, 256, 256], P(('row', 'rep')), as said below
- tile_rows: int32 [8192], P(('row', 'rep')), may hold values from 0 to 127, as said below
- tile_cols: int32 [8192], P(('row', 'rep')), may hold values from 0 to 127, as said below
Outputs:
- directions: float32 [32, 524288], P(None, ('row', 'rep'))
- projected: float32 [64, 64], replicated
Inputs may be any that keep to these rules, and one draw needn't show every extreme that they name: The matrix A assembled from all tiles as the steps say is symmetric. `tile_rows`: each device's 32 entries index tile-rows of its band, which are held by the devices of its index along row, in the order of rep. The first 8 entries of a device are its diagonal tiles: the t-th is (index along rep) * 8 + t. Of the other entries none falls in the device's own index along rep, and at most 2 fall in the tile-rows of any one other index along rep, exactly 2 for some. `tile_cols`: each device's 32 entries index tile-columns held by the devices of its index along rep, in the order of row. The first 8 entries of a device are (index along row) * 8 + t for the t-th. Of the other entries none falls in the device's own index along row, and at most 2 fall in the tile-columns of any one other index along row, exactly 2 for some.
All inputs are finite; a program needn't handle non-finite values.
Results may differ from a plain program's by a relative error of at most 0.0003.
Values sent between devices are 32-bit elements; how exact they have to be, the bound alone decides.
A program may use at most 64 MiB of HBM per device.

v0:
```python
import jax
import jax.numpy as jnp
from jax import lax
from jax.sharding import Mesh
from jax.sharding import PartitionSpec as P

ROW = ("row_0", "row_1")
REP = ("rep_0", "rep_1")
ROW_REP = ("row_0", "row_1", "rep_0", "rep_1")


def from_everyone(shard, axis):
    size = lax.axis_size(axis)
    return lax.all_to_all(
        jnp.broadcast_to(shard[None], (size, *shard.shape)), axis, 0, 0, tiled=True
    )


def over_copies(shard, axis):
    everything = from_everyone(shard, axis)
    return jnp.sum(everything, axis=0)


def over_axes(shard, axes):
    far, near = axes
    nearer = over_copies(shard, near)
    return over_copies(nearer, far)


def together(arrays, axis):
    ends = [0]
    for a in arrays:
        ends.append(ends[-1] + a.size)
    total = over_axes(jnp.concatenate([a.ravel() for a in arrays]), axis)
    return tuple((total[b:e].reshape(a.shape) for a, b, e in zip(arrays, ends, ends[1:])))


def slot_ranks(peers, peer_count):
    peer_hot = (peers[:, None] == jnp.arange(peer_count, dtype=jnp.int32)[None, :]).astype(
        jnp.int32
    )
    before = jnp.cumsum(peer_hot, axis=0) - peer_hot
    return jnp.sum(before * peer_hot, axis=1)


def shards(basis, precond, tiles, tile_rows, tile_cols):
    highest = lax.Precision.HIGHEST
    columns = basis.shape[0]
    shard_rows = basis.shape[1]
    tile_size = tiles.shape[1]
    tiles_each = shard_rows // tile_size
    row_count = lax.axis_size(ROW)
    rep_count = lax.axis_size(REP)
    inverse_count = 1.0 / (shard_rows * row_count * rep_count)
    basis_float = basis.astype(jnp.float32)
    pairs_here = (tile_rows.shape[0] - tiles_each) // 2
    most_col = 2 * ((pairs_here + row_count - 2) // (row_count - 1))
    most_row = 2 * ((pairs_here + rep_count - 2) // (rep_count - 1))
    other_cols = tile_cols[tiles_each:]
    col_peer = other_cols // tiles_each
    col_local = other_cols % tiles_each
    col_slot = col_peer * most_col + slot_ranks(col_peer, row_count)
    col_hot = (
        col_slot[:, None] == jnp.arange(row_count * most_col, dtype=jnp.int32)[None, :]
    ).astype(jnp.int32)
    requests = jnp.sum(col_hot * col_local[:, None], axis=0)
    wanted = lax.all_to_all(requests, ROW, split_axis=0, concat_axis=0, tiled=True)
    other_rows = tile_rows[tiles_each:]
    row_peer = other_rows // tiles_each
    row_local = other_rows % tiles_each
    row_slot = row_peer * most_row + slot_ranks(row_peer, rep_count)
    slot_hot = row_slot[:, None] == jnp.arange(rep_count * most_row, dtype=jnp.int32)[None, :]
    slot_map = slot_hot.astype(jnp.float32)
    target_rows = jnp.sum(slot_hot.astype(jnp.int32) * row_local[:, None], axis=0)[None, :]
    own_rows_index = jnp.arange(tiles_each, dtype=jnp.int32)

    def apply_matrix(vectors):
        own_blocks = vectors.reshape(columns, tiles_each, tile_size)
        outgoing = jnp.take(own_blocks, wanted, axis=1)
        fetched = lax.all_to_all(outgoing, ROW, split_axis=1, concat_axis=1, tiled=True)
        diagonal_products = jnp.einsum(
            "ktc,trc->ktr",
            own_blocks,
            tiles[:tiles_each],
            precision=highest,
            preferred_element_type=jnp.float32,
        )
        picked = jnp.take(fetched, col_slot, axis=1)
        other_products = jnp.einsum(
            "kjc,jrc->kjr",
            picked,
            tiles[tiles_each:],
            precision=highest,
            preferred_element_type=jnp.float32,
        )
        packed = jnp.einsum("kjr,js->ksr", other_products, slot_map, precision=highest)
        incoming, arrived_rows = (
            lax.all_to_all(packed, REP, split_axis=1, concat_axis=1, tiled=True),
            lax.all_to_all(target_rows, REP, split_axis=1, concat_axis=1, tiled=True),
        )
        arrive_map = (arrived_rows[0][:, None] == own_rows_index[None, :]).astype(jnp.float32)
        received = jnp.einsum("ksr,st->ktr", incoming, arrive_map, precision=highest)
        summed = (diagonal_products + received).reshape(columns, -1)
        return summed

    applied = apply_matrix(basis_float)
    basis_applied, basis_gram, scaled_applied, scaled_gram = together(
        (
            jnp.dot(applied, basis_float.T, precision=highest),
            jnp.dot(basis_float, basis_float.T, precision=highest),
            jnp.dot(precond[None, :] * applied, basis_float.T, precision=highest),
            jnp.dot(precond[None, :] * basis_float, basis_float.T, precision=highest),
        ),
        ("row_0", ("row_1", "rep_0", "rep_1")),
    )
    basis_applied = basis_applied * inverse_count
    basis_gram = basis_gram * inverse_count
    scaled_applied = scaled_applied * inverse_count
    scaled_gram = scaled_gram * inverse_count
    ritz_values = jnp.diagonal(basis_applied)
    residual = applied - ritz_values[:, None] * basis_float
    correlation = basis_applied - ritz_values[:, None] * basis_gram
    right_side = -(residual - jnp.dot(correlation, basis_float, precision=highest))
    seeded = precond[None, :] * right_side
    coefficients = (
        -scaled_applied
        + ritz_values[:, None] * scaled_gram
        + jnp.dot(correlation, scaled_gram, precision=highest)
    )
    correction = seeded - jnp.dot(coefficients, basis_float, precision=highest)
    image_block = apply_matrix(correction)
    updated = correction + precond[None, :] * (
        right_side - (image_block - ritz_values[:, None] * correction)
    )
    coefficients = (
        over_axes(
            jnp.dot(updated, basis_float.T, precision=highest),
            (("row_0", "row_1", "rep_0"), "rep_1"),
        )
        * inverse_count
    )
    correction = updated - jnp.dot(coefficients, basis_float, precision=highest)
    correction_gram = (
        over_axes(
            jnp.dot(correction, correction.T, precision=highest),
            (("row_0", "row_1", "rep_0"), "rep_1"),
        )
        * inverse_count
    )
    factor = jnp.linalg.cholesky(correction_gram)
    directions = lax.linalg.triangular_solve(factor, correction, left_side=True, lower=True)
    adirections = apply_matrix(directions)
    block_cross, block_new = together(
        (
            jnp.dot(basis_float, adirections.T, precision=highest),
            jnp.dot(directions, adirections.T, precision=highest),
        ),
        (("row_0", "row_1", "rep_0"), "rep_1"),
    )
    block_basis = basis_applied.T
    block_cross = block_cross * inverse_count
    block_new = block_new * inverse_count
    upper = jnp.concatenate([block_basis, block_cross], axis=1)
    lower = jnp.concatenate([block_cross.T, block_new], axis=1)
    projected = jnp.concatenate([upper, lower], axis=0)
    return (directions, projected)


def solution(mesh):
    split = Mesh(mesh.devices.reshape(8, 2, 4, 4), ("row_0", "row_1", "rep_0", "rep_1"))
    placed = (P(None, ROW_REP), P(ROW_REP), P(ROW_REP, None, None), P(ROW_REP), P(ROW_REP))
    return jax.shard_map(
        shards, mesh=split, in_specs=placed, out_specs=(P(None, ROW_REP), P()), check_vma=False
    )
```

profile of v0, /device:TPU:1, one launch (start us, length us, event | category | flops | bytes accessed | tf_op | source)
XLA Modules:
  0.0 354.2 jit_solution(16680483082879712353)
XLA Ops:
  2.5 10.0 %all-to-all-start.1 = ((s32[16,2,1]{1,2,0:T(1,128)}), s32[16,2,1]{1,2,0:T(1,128)S(1)}, u32[]{:S(2)}, u32[]{:S(2)}) async-start(s32[16,2,1]{1,2,0:T(1,128)} %bitcast.4), calls=%async_computation.1 | async-start | bytes 16384 | tf_op jit(solution)/shard_map/all_to_all | solution.py:67
  13.4 6.0 %all-to-all-done.1 = s32[16,2,1]{1,2,0:T(1,128)S(1)} async-done(((s32[16,2,1]{1,2,0:T(1,128)}), s32[16,2,1]{1,2,0:T(1,128)S(1)}, u32[]{:S(2)}, u32[]{:S(2)}) %all-to-all-start.1) | async-done | bytes 160 | tf_op jit(solution)/shard_map/all_to_all | solution.py:67
  22.5 4.1 %all-to-all-start.2 = ((f32[32,32,256]{2,0,1:T(8,128)}), f32[32,32,256]{2,0,1:T(8,128)S(1)}, u32[]{:S(2)}, u32[]{:S(2)}) async-start(f32[32,32,256]{2,0,1:T(8,128)} %select_bitcast_fusion.2), calls=%async_computation.2 | async-start | bytes 2097152 | tf_op jit(solution)/shard_map/all_to_all | solution.py:80
  27.9 26.8 %all-to-all-done.2 = f32[32,32,256]{2,0,1:T(8,128)S(1)} async-done(((f32[32,32,256]{2,0,1:T(8,128)}), f32[32,32,256]{2,0,1:T(8,128)S(1)}, u32[]{:S(2)}, u32[]{:S(2)}) %all-to-all-start.2) | async-done | bytes 1048608 | tf_op jit(solution)/shard_map/all_to_all | solution.py:80
  54.6 6.8 %all-to-all-start = ((s32[1,16,2]{2,0,1:T(1,128)}), s32[1,16,2]{2,0,1:T(1,128)S(1)}, u32[]{:S(2)}, u32[]{:S(2)}) async-start(s32[1,16,2]{2,0,1:T(1,128)} %bitcast.1), calls=%async_computation | async-start | bytes 16384 | tf_op jit(solution)/shard_map/all_to_all | solution.py:99
  62.0 4.7 %fusion.7 = f32[32,24,256]{2,0,1:T(8,128)S(1)} fusion(bf16[32,256,256]{2,1,0:T(8,128)(2,1)} %param.11, f32[24,32,256]{2,1,0:T(8,128)S(1)} %gather_fusion.2, pred[24]{0:T(512)(128)(4,1)S(1)} %get-tuple-element.16), kind=kOutput, calls=%fused_computation.20 | convolution fusion | flops 604176384 | bytes 4718616 | tf_op jit(solution)/shard_map/kjc,jrc->kjr/dot_general | solution.py:89
  66.8 1.1 convolution_bitcast_fusion.2
  67.9 1.6 copy.113
  69.5 6.7 %all-to-all-start.3 = ((f32[32,32,256]{2,0,1:T(8,128)}), f32[32,32,256]{2,0,1:T(8,128)S(1)}, u32[]{:S(2)}, u32[]{:S(2)}) async-start(f32[32,32,256]{2,0,1:T(8,128)} %copy.113), calls=%async_computation.3 | async-start | bytes 2097152 | tf_op jit(solution)/shard_map/all_to_all | solution.py:98
  77.5 17.0 %all-to-all-done.3 = f32[32,32,256]{2,0,1:T(8,128)S(1)} async-done(((f32[32,32,256]{2,0,1:T(8,128)}), f32[32,32,256]{2,0,1:T(8,128)S(1)}, u32[]{:S(2)}, u32[]{:S(2)}) %all-to-all-start.3) | async-done | bytes 1048608 | tf_op jit(solution)/shard_map/all_to_all | solution.py:98
  95.6 1.6 fusion.17
  98.4 15.1 %all_to_all.97 = f32[32,1,4096]{2,1,0:T(1,128)S(1)} all-to-all(f32[32,1,4096]{2,1,0:T(1,128)S(1)} %broadcast_in_dim.39), channel_id=1, replica_groups=mesh['row_0'=8,'row_1'=2,'rep_0'=4,'rep_1'=4] {'row_1','rep_0','rep_1'}, dimensions={0} | all-to-all | bytes 1048576 | tf_op jit(solution)/shard_map/all_to_all | solution.py:14
  114.5 3.4 all-to-all-start.5
  117.9 7.9 %all-to-all-done.5 = f32[8,1,4096]{2,1,0:T(1,128)S(1)} async-done(((f32[8,1,4096]{2,1,0:T(1,128)}), f32[8,1,4096]{2,1,0:T(1,128)S(1)}, u32[]{:S(2)}, u32[]{:S(2)}) %all-to-all-start.5) | async-done | bytes 131104 | tf_op jit(solution)/shard_map/all_to_all | solution.py:14
  128.6 33.3 %all_to_all.98 = f32[32,32,256]{2,0,1:T(8,128)S(1)} all-to-all(f32[32,32,256]{2,0,1:T(8,128)S(1)} %select_bitcast_fusion.1), channel_id=1, replica_groups=mesh['row_0'=8,'row_1'=2,'rep_0'=4,'rep_1'=4] {'row_0','row_1'}, dimensions={1} | all-to-all | bytes 2097152 | tf_op jit(solution)/shard_map/all_to_all | solution.py:80
  162.5 4.7 %fusion.10 = f32[32,24,256]{2,0,1:T(8,128)S(1)} fusion(bf16[32,256,256]{2,1,0:T(8,128)(2,1)} %param.11, f32[24,32,256]{2,1,0:T(8,128)S(1)} %gather_fusion.4, pred[24]{0:T(512)(128)(4,1)S(1)} %get-tuple-element.16), kind=kOutput, calls=%fused_computation.21 | convolution fusion | flops 604176384 | bytes 4718616 | tf_op jit(solution)/shard_map/kjc,jrc->kjr/dot_general | solution.py:89
  169.0 20.2 %all_to_all.99 = f32[32,32,256]{2,0,1:T(8,128)S(1)} all-to-all(f32[32,32,256]{2,0,1:T(8,128)S(1)} %copy.122), channel_id=1, replica_groups=mesh['row_0'=8,'row_1'=2,'rep_0'=4,'rep_1'=4] {'rep_0','rep_1'}, dimensions={1} | all-to-all | bytes 2097152 | tf_op jit(solution)/shard_map/all_to_all | solution.py:98
  190.2 2.2 fusion.19
  192.9 6.6 %all_to_all.100 = f32[4,1,1024]{2,1,0:T(1,128)S(1)} all-to-all(f32[4,1,1024]{2,1,0:T(1,128)S(1)} %reshape.270), channel_id=1, replica_groups=mesh['row_0'=8,'row_1'=2,'rep_0'=4,'rep_1'=4] {'rep_1'}, dimensions={0} | all-to-all | bytes 32768 | tf_op jit(solution)/shard_map/all_to_all | solution.py:14
  201.4 18.2 %all_to_all.101 = f32[64,1,1024]{2,1,0:T(1,128)S(1)} all-to-all(f32[64,1,1024]{2,1,0:T(1,128)S(1)} %reshape.272), channel_id=1, replica_groups=mesh['row_0'=8,'row_1'=2,'rep_0'=4,'rep_1'=4] {'row_0','row_1','rep_0'}, dimensions={0} | all-to-all | bytes 524288 | tf_op jit(solution)/shard_map/all_to_all | solution.py:14
  219.6 1.3 reduce.19
  222.0 6.6 %all_to_all.102 = f32[4,1,1024]{2,1,0:T(1,128)S(1)} all-to-all(f32[4,1,1024]{2,1,0:T(1,128)S(1)} %reshape.274), channel_id=1, replica_groups=mesh['row_0'=8,'row_1'=2,'rep_0'=4,'rep_1'=4] {'rep_1'}, dimensions={0} | all-to-all | bytes 32768 | tf_op jit(solution)/shard_map/all_to_all | solution.py:14
  230.0 18.8 %all_to_all.103 = f32[64,1,1024]{2,1,0:T(1,128)S(1)} all-to-all(f32[64,1,1024]{2,1,0:T(1,128)S(1)} %reshape.276), channel_id=1, replica_groups=mesh['row_0'=8,'row_1'=2,'rep_0'=4,'rep_1'=4] {'row_0','row_1','rep_0'}, dimensions={0} | all-to-all | bytes 524288 | tf_op jit(solution)/shard_map/all_to_all | solution.py:14
  248.8 1.3 reduce.21
  250.6 2.9 cholesky.16
  254.8 2.4 custom-call.6
  258.5 33.0 %all_to_all.104 = f32[32,32,256]{2,0,1:T(8,128)S(1)} all-to-all(f32[32,32,256]{2,0,1:T(8,128)S(1)} %select_bitcast_fusion), channel_id=1, replica_groups=mesh['row_0'=8,'row_1'=2,'rep_0'=4,'rep_1'=4] {'row_0','row_1'}, dimensions={1} | all-to-all | bytes 2097152 | tf_op jit(solution)/shard_map/all_to_all | solution.py:80
  292.1 4.7 %fusion.13 = f32[32,24,256]{2,0,1:T(8,128)S(1)} fusion(bf16[32,256,256]{2,1,0:T(8,128)(2,1)} %param.11, f32[24,32,256]{2,1,0:T(8,128)S(1)} %gather_fusion.6, pred[24]{0:T(512)(128)(4,1)S(1)} %get-tuple-element.16), kind=kOutput, calls=%fused_computation.22 | convolution fusion | flops 604176384 | bytes 4718616 | tf_op jit(solution)/shard_map/kjc,jrc->kjr/dot_general | solution.py:89
  298.6 19.9 %all_to_all.105 = f32[32,32,256]{2,0,1:T(8,128)S(1)} all-to-all(f32[32,32,256]{2,0,1:T(8,128)S(1)} %copy.132), channel_id=1, replica_groups=mesh['row_0'=8,'row_1'=2,'rep_0'=4,'rep_1'=4] {'rep_0','rep_1'}, dimensions={1} | all-to-all | bytes 2097152 | tf_op jit(solution)/shard_map/all_to_all | solution.py:98
  319.6 2.2 fusion.18
  322.7 6.7 %all_to_all.106 = f32[4,1,2048]{2,1,0:T(1,128)S(1)} all-to-all(f32[4,1,2048]{2,1,0:T(1,128)S(1)} %broadcast_in_dim.45), channel_id=1, replica_groups=mesh['row_0'=8,'row_1'=2,'rep_0'=4,'rep_1'=4] {'rep_1'}, dimensions={0} | all-to-all | bytes 65536 | tf_op jit(solution)/shard_map/all_to_all | solution.py:14
  329.7 23.0 %all_to_all.107 = f32[64,1,2048]{2,1,0:T(1,128)S(1)} all-to-all(f32[64,1,2048]{2,1,0:T(1,128)S(1)} %broadcast_in_dim.46), channel_id=1, replica_groups=mesh['row_0'=8,'row_1'=2,'rep_0'=4,'rep_1'=4] {'row_0','row_1','rep_0'}, dimensions={0} | all-to-all | bytes 1048576 | tf_op jit(solution)/shard_map/all_to_all | solution.py:14
  (128 shorter events, 32.2 us)
Async XLA Ops:
  0.6 26.0 %copy-start.3 = (s32[32]{0:T(128)S(1)}, s32[32]{0:T(128)}, u32[]{:S(2)}) copy-start(s32[32]{0:T(128)} %param.12) | copy-start | bytes 388
  2.5 16.9 %all-to-all-start.1 = ((s32[16,2,1]{1,2,0:T(1,128)}), s32[16,2,1]{1,2,0:T(1,128)S(1)}, u32[]{:S(2)}, u32[]{:S(2)}) async-start(s32[16,2,1]{1,2,0:T(1,128)} %bitcast.4), calls=%async_computation.1 | async-start | bytes 16384 | tf_op jit(solution)/shard_map/all_to_all | solution.py:67
  22.5 32.1 %all-to-all-start.2 = ((f32[32,32,256]{2,0,1:T(8,128)}), f32[32,32,256]{2,0,1:T(8,128)S(1)}, u32[]{:S(2)}, u32[]{:S(2)}) async-start(f32[32,32,256]{2,0,1:T(8,128)} %select_bitcast_fusion.2), calls=%async_computation.2 | async-start | bytes 2097152 | tf_op jit(solution)/shard_map/all_to_all | solution.py:80
  54.6 14.9 %all-to-all-start = ((s32[1,16,2]{2,0,1:T(1,128)}), s32[1,16,2]{2,0,1:T(1,128)S(1)}, u32[]{:S(2)}, u32[]{:S(2)}) async-start(s32[1,16,2]{2,0,1:T(1,128)} %bitcast.1), calls=%async_computation | async-start | bytes 16384 | tf_op jit(solution)/shard_map/all_to_all | solution.py:99
  66.7 9.4 %copy-start = (bf16[32,2048]{1,0:T(8,128)(2,1)S(1)}, bf16[32,2048]{1,0:T(8,128)(2,1)}, u32[]{:S(2)}) copy-start(bf16[32,2048]{1,0:T(8,128)(2,1)} %param.9) | copy-start | bytes 393220
  66.8 9.7 %copy-start.2 = (f32[2048]{0:T(1024)S(1)}, f32[2048]{0:T(1024)}, u32[]{:S(2)}) copy-start(f32[2048]{0:T(1024)} %param.10) | copy-start | bytes 24580
  69.5 25.0 %all-to-all-start.3 = ((f32[32,32,256]{2,0,1:T(8,128)}), f32[32,32,256]{2,0,1:T(8,128)S(1)}, u32[]{:S(2)}, u32[]{:S(2)}) async-start(f32[32,32,256]{2,0,1:T(8,128)} %copy.113), calls=%async_computation.3 | async-start | bytes 2097152 | tf_op jit(solution)/shard_map/all_to_all | solution.py:98
  114.5 11.3 %all-to-all-start.5 = ((f32[8,1,4096]{2,1,0:T(1,128)}), f32[8,1,4096]{2,1,0:T(1,128)S(1)}, u32[]{:S(2)}, u32[]{:S(2)}) async-start(f32[8,1,4096]{2,1,0:T(1,128)} %broadcast_in_dim.40), calls=%async_computation.5 | async-start | bytes 262144 | tf_op jit(solution)/shard_map/all_to_all | solution.py:14
  257.7 64.4 %copy-start.1 = (f32[32,2048]{1,0:T(8,128)}, f32[32,2048]{1,0:T(8,128)S(1)}, u32[]{:S(2)}) copy-start(f32[32,2048]{1,0:T(8,128)S(1)} %fusion.53) | copy-start | bytes 786436
where the time goes:
time: 355 us; the launch traced here: 354 us
  blocking collectives  201 us (57%)
  waiting for transfers between devices  57.7 us (16%)
  starting transfers between devices  30.9 us (9%)
  matrix products  30.3 us (9%)
  other arithmetic  17.3 us (5%)
  local copies, waits for them, and re-layouts  15.4 us (4%)
    all_to_all x7, blocking collectives, from_everyone(): lax.all_to_all(jnp.broadcast_to(shard[None], (size, *shard.shape)), axis,...  94.9 us
    all_to_all x2, blocking collectives, apply_matrix(): lax.all_to_all(outgoing, ROW, split_axis=1, concat_axis=1, tiled=True)  66.3 us
    all_to_all x2, blocking collectives, apply_matrix(): lax.all_to_all(packed, REP, split_axis=1, concat_axis=1, tiled=True)  40.1 us
    all_to_all x1, waiting for transfers between devices, apply_matrix(): lax.all_to_all(outgoing, ROW, split_axis=1, concat_axis=1, tiled=True)  26.8 us
    all_to_all x1, waiting for transfers between devices, apply_matrix(): lax.all_to_all(packed, REP, split_axis=1, concat_axis=1, tiled=True)  17 us
    dot_general x3, matrix products, apply_matrix(): jnp.einsum('kjc,jrc->kjr', picked, tiles[tiles_each:], precision=highest,...  14.2 us
    all_to_all x1, starting transfers between devices, shards(): lax.all_to_all(requests, ROW, split_axis=0, concat_axis=0, tiled=True)  9.97 us
    all_to_all x1, waiting for transfers between devices, from_everyone(): lax.all_to_all(jnp.broadcast_to(shard[None], (size, *shard.shape)), axis,...  7.92 us
  transfers between devices with their start and end apart: 5, of which 4 were waited for; matrix products, arithmetic and copies ran while one was open for 3% of the time, Pallas kernels for 0%

commit v1 on v0

v1 whole, which is shorter than its diff:
```python
import functools
import jax
import jax.numpy as jnp
from jax import lax
from jax.experimental import pallas as pl
from jax.experimental.pallas import tpu as pltpu
from jax.sharding import PartitionSpec as P

MESH = pl.DeviceIdType.MESH
F32 = jnp.float32
BF16 = jnp.bfloat16
HIGHEST = lax.Precision.HIGHEST


def fetches(me, peer_core, delta, chips):
    same = peer_core == me % 2
    half = chips // 2
    straight = (delta < half) | ((delta == half) & (me // 2 < half))
    return (delta == 0) | (same == straight)


def request_table(tile_rows, tile_cols, each, rows, reps):
    row = lax.axis_index("row")
    rep = lax.axis_index("rep")
    chips = rows // 2
    other_rows = tile_rows[each:]
    other_cols = tile_cols[each:]
    col_peer = other_cols // each
    row_peer = other_rows // each
    delta = lax.rem(col_peer // 2 - row // 2 + chips, chips)
    chosen = fetches(row, col_peer % 2, delta, chips)
    place = jnp.arange(other_rows.shape[0], dtype=jnp.int32)
    earlier = place[None, :] < place[:, None]
    col_rank = jnp.sum(
        (earlier & (col_peer[:, None] == col_peer[None, :])).astype(jnp.int32), axis=1
    )
    row_rank = jnp.sum(
        (earlier & chosen[None, :] & (row_peer[:, None] == row_peer[None, :])).astype(jnp.int32),
        axis=1,
    )
    z_slot = 2 * delta + col_rank
    x_slot = 2 * (lax.rem(row_peer - rep + reps, reps) - 1) + row_rank
    z_code = (each + place) + x_slot * 256 + (other_cols % each) * 65536 + 16777216
    x_code = z_slot + (other_rows % each) * 65536 + 16777216
    z_slot = jnp.where(chosen, z_slot, -1)
    x_slot = jnp.where(chosen, x_slot + 2 * chips, -1)
    slots = jnp.arange(2 * (chips + reps - 1), dtype=jnp.int32)
    slots = jnp.broadcast_to(slots[:, None, None], (slots.shape[0], 128, 1))
    code = jnp.sum(
        jnp.where(slots == z_slot, z_code, 0) + jnp.where(slots == x_slot, x_code, 0), axis=2
    )
    code = jnp.where(code == 0, each * 65536, code)
    return code.reshape(chips + reps - 1, 2, 128)


def split(x):
    high = x.astype(BF16)
    low = (x - high.astype(F32)).astype(BF16)
    return high, low


def stacked(x):
    return jnp.concatenate(split(x), axis=0)


def folded(x):
    half = x.shape[0] // 2
    return x[:half] + x[half:]


def dot(a, b):
    return lax.dot_general(a, b, (((1,), (0,)), ((), ())), preferred_element_type=F32)


def dot_t(a, b):
    return lax.dot_general(a, b, (((1,), (1,)), ((), ())), preferred_element_type=F32)


def exact(a, b):
    return lax.dot_general(
        a, b, (((1,), (0,)), ((), ())), precision=HIGHEST, preferred_element_type=F32
    )


def exact_t(a, b):
    return lax.dot_general(
        a, b, (((1,), (1,)), ((), ())), precision=HIGHEST, preferred_element_type=F32
    )


def inverse_factor(gram):
    n = gram.shape[0]
    row_of = lax.broadcasted_iota(jnp.int32, (n, n), 0)
    col_of = lax.broadcasted_iota(jnp.int32, (n, n), 1)
    work = jnp.concatenate([gram, (row_of == col_of).astype(F32)], axis=1)
    which = lax.broadcasted_iota(jnp.int32, (n, 1), 0)
    for j in range(n):
        scale = lax.rsqrt(work[j : j + 1, j : j + 1])
        pivot = work[j : j + 1, :] * scale
        ratio = work[:, j : j + 1] * scale
        work = jnp.where(
            which == j, pivot, work - jnp.where(which > j, ratio, 0.0) * pivot
        )
    return work[:, n:]


def kernel(
    rows,
    reps,
    scale,
    codes,
    request,
    basis,
    precond,
    tiles_far,
    directions,
    projected,
    tiles,
    wanted,
    wants,
    base,
    weight,
    weight_sz,
    weight_sx,
    weight_rz,
    weight_rx,
    sz1,
    sx1,
    rz1,
    rx1,
    sz2,
    sx2,
    rz2,
    rx2,
    sz3,
    sx3,
    rz3,
    rx3,
    prod_i,
    prod_j1,
    prod_j2,
    tx1,
    tx2,
    bz1,
    bx1,
    bz2,
    bx2,
    diag,
    applied,
    right,
    seed,
    updated,
    m1,
    a1,
    b1,
    c1,
    m2,
    a2,
    b2,
    c2,
    piece,
    gathered,
    m3,
    a3,
    b3,
    small,
    send,
    recv,
    local,
):
    row = lax.axis_index("row")
    rep = lax.axis_index("rep")
    chips = rows // 2
    each = base.shape[0]
    size = base.shape[2]
    count = base.shape[1]
    z_slots = 2 * chips
    x_slots = 2 * (reps - 1)
    chip = row // 2
    core = lax.rem(row, 2)

    diag_load = pltpu.make_async_copy(
        tiles_far.at[pl.ds(0, each)], tiles.at[pl.ds(0, each)], local.at[0]
    )
    rest = tiles.shape[0] - each
    other_load = pltpu.make_async_copy(
        tiles_far.at[pl.ds(each, rest)], tiles.at[pl.ds(each, rest)], local.at[1]
    )
    diag_load.start()
    other_load.start()

    barrier = pltpu.get_barrier_semaphore()
    for d in range(1, rows):
        pl.semaphore_signal(
            barrier, inc=1, device_id={"row": lax.rem(row + d, rows)}, device_id_type=MESH
        )
    for d in range(1, reps):
        pl.semaphore_signal(
            barrier, inc=1, device_id={"rep": lax.rem(rep + d, reps)}, device_id_type=MESH
        )

    def z_holder(delta):
        half = chips // 2
        if delta == 0:
            other = 1 - core
        elif delta < half:
            other = core
        elif delta > half:
            other = 1 - core
        else:
            other = jnp.where(chip < half, core, 1 - core)
        return {"row": lax.rem(chip + delta, chips) * 2 + other}

    def z_reader(delta):
        half = chips // 2
        there = lax.rem(chip - delta + chips, chips)
        if delta == 0:
            other = 1 - core
        elif delta < half:
            other = core
        elif delta > half:
            other = 1 - core
        else:
            other = jnp.where(there < half, core, 1 - core)
        return {"row": there * 2 + other}

    def x_holder(sigma):
        return {"rep": lax.rem(rep + sigma, reps)}

    def x_reader(sigma):
        return {"rep": lax.rem(rep - sigma + reps, reps)}

    def push(source, target, key, device):
        pltpu.make_async_remote_copy(
            src_ref=source,
            dst_ref=target,
            send_sem=send.at[key],
            recv_sem=recv.at[key],
            device_id=device,
            device_id_type=MESH,
        ).start()

    def landed(buffer, key):
        pltpu.make_async_copy(buffer, buffer, recv.at[key]).wait()

    def gone(buffer, key):
        pltpu.make_async_copy(buffer, buffer, send.at[key]).wait()

    for t in range(each):
        base[t] = basis[:, t * size : (t + 1) * size].astype(F32)
        weight[t] = precond[:, t * size : (t + 1) * size]

    pl.semaphore_wait(barrier, rows + reps - 2)

    for delta in range(chips):
        push(request.at[delta], wanted.at[delta], 0, z_holder(delta))
    for sigma in range(1, reps):
        push(request.at[chips + sigma - 1], wanted.at[chips + sigma - 1], 0, x_holder(sigma))

    diag_load.wait()
    for t in range(each):
        diag[t] = dot_t(basis[:, t * size : (t + 1) * size], tiles[t])

    landed(wanted, 0)
    to_scalars = pltpu.make_async_copy(wanted, wants, local.at[2])
    to_scalars.start()
    to_scalars.wait()

    def z_asked(slot):
        return (wants[slot // 2, slot % 2, 0] // 65536) % each

    def x_asked(slot):
        return (wants[chips + slot // 2, slot % 2, 0] // 65536) % each

    def pack(source, to_z, to_x):
        for slot in range(z_slots):
            to_z[slot] = source[z_asked(slot)]
        for slot in range(x_slots):
            to_x[slot] = source[x_asked(slot)]

    def fetch_steps(from_z, from_x, to_z, to_x, key):
        def z_step(delta):
            part = pl.ds(2 * delta, 2)
            return lambda: push(from_z.at[part], to_z.at[part], key, z_reader(delta))

        def x_step(sigma):
            part = pl.ds(2 * (sigma - 1), 2)
            return lambda: push(from_x.at[part], to_x.at[part], key + 1, x_reader(sigma))

        half = chips // 2
        z_order = sorted(range(chips), key=lambda delta: -min(delta, chips - delta))
        z_steps = [z_step(delta) for delta in z_order]
        x_steps = [x_step(sigma) for sigma in range(1, reps)]
        steps = []
        while z_steps or x_steps:
            steps += x_steps[:2] + z_steps[:1]
            x_steps = x_steps[2:]
            z_steps = z_steps[1:]
        return steps

    def z_code(slot):
        return codes[slot // 2, slot % 2, 0]

    def tile_of(slot):
        return tiles[z_code(slot) % 256]

    def x_of(slot):
        return (z_code(slot) // 256) % 256

    def x_source(slot):
        return codes[chips + slot // 2, slot % 2, 0] % 256

    def return_steps(parts_i, parts_j, images, packed, to_z, to_x, key):
        for slot in range(z_slots):
            images[slot] = parts_i(slot)
        for slot in range(x_slots):
            packed[slot] = images[x_source(slot)]
        for sigma in range(1, reps):
            part = pl.ds(2 * (sigma - 1), 2)
            push(packed.at[part], to_x.at[part], key + 1, x_holder(sigma))
        for delta in range(1, chips):
            for slot in (2 * delta, 2 * delta + 1):
                parts_j[1][slot] = parts_j[0](slot)
            part = pl.ds(2 * delta, 2)
            push(parts_j[1].at[part], to_z.at[part], key, z_holder(delta))

    def summed(from_z, from_x, target):
        def strip(index, carry):
            begin = pl.multiple_of(index * 8, 8)
            here = pl.ds(begin, 8)
            totals = [diag[t, here, :] for t in range(each)]
            slots = [(from_z, slot, slot // 2, slot % 2) for slot in range(2, z_slots)]
            slots += [
                (from_x, slot, chips + slot // 2, slot % 2) for slot in range(x_slots)
            ]
            for source, slot, peer, place in slots:
                value = source[slot, here, :]
                asked = wanted[peer, place : place + 1, :] // 65536
                for t in range(each):
                    hit = jnp.broadcast_to(asked % 256 == t, (8, 128))
                    hit = jnp.concatenate([hit] * (size // 128), axis=1)
                    totals[t] = totals[t] + jnp.where(hit, value, 0.0)
            for t in range(each):
                target[t, here, :] = totals[t]
            return carry

        lax.fori_loop(0, count // 8, strip, 0)

    def scatter(full, slots, key):
        for d in range(1, rows):
            to = lax.rem(row + d, rows)
            push(full.at[to], slots.at[row], key, {"row": to})
        pltpu.make_async_copy(full.at[row], slots.at[row], recv.at[key]).start()

    def spread(source, slots, key, axis):
        if axis == "row":
            me, length = row, rows
        else:
            me, length = rep, reps
        for d in range(1, length):
            push(source, slots.at[me], key, {axis: lax.rem(me + d, length)})
        pltpu.make_async_copy(source, slots.at[me], recv.at[key]).start()

    def total(slots):
        value = slots[0]
        for i in range(1, slots.shape[0]):
            value = value + slots[i]
        return value

    def reduce_steps(value, full, slots_a, slots_b, slots_c, key, out, which, fillers):
        part = value.shape[0] // rows
        for i in range(rows):
            full[i] = value[i * part : (i + 1) * part, :]
        scatter(full, slots_a, key)
        fillers[0]()
        landed(slots_a, key)
        piece[which] = total(slots_a)
        spread(piece.at[which], slots_b, key + 1, "rep")
        fillers[1]()
        landed(slots_b, key + 1)
        piece[which + 1] = total(slots_b)
        spread(piece.at[which + 1], slots_c, key + 2, "row")
        fillers[2]()
        landed(slots_c, key + 2)
        for i in range(rows):
            out[i * part : (i + 1) * part, :] = slots_c[i]

    pack(base, sz1, sx1)
    for slot in range(z_slots):
        weight_sz[slot] = weight[z_asked(slot)]
    for slot in range(x_slots):
        weight_sx[slot] = weight[x_asked(slot)]
    for step in fetch_steps(sz1, sx1, rz1, rx1, 1):
        step()
    for step in fetch_steps(weight_sz, weight_sx, weight_rz, weight_rx, 3):
        step()
    other_load.wait()
    landed(rz1, 1)
    landed(rx1, 2)
    return_steps(
        lambda slot: dot_t(rz1[slot].astype(BF16), tile_of(slot)),
        (lambda slot: dot(rx1[x_of(slot)].astype(BF16), tile_of(slot)), prod_j1),
        prod_i,
        tx1,
        bz1,
        bx1,
        5,
    )
    landed(bz1.at[pl.ds(2, z_slots - 2)], 5)
    landed(bx1, 6)
    summed(bz1, bx1, applied)

    pack(applied, sz2, sx2)
    steps = fetch_steps(sz2, sx2, rz2, rx2, 7)
    third = (len(steps) + 3) // 4
    for step in steps[:third]:
        step()
    first = jnp.zeros((3 * count, 3 * count), F32)
    for t in range(each):
        block = base[t]
        basis_part = block.astype(BF16)
        first = first + dot_t(
            jnp.concatenate([*split(applied[t]), basis_part], axis=0),
            jnp.concatenate([basis_part, *split(block * weight[t])], axis=0),
        )
    first = jnp.concatenate([first[:count] + first[count : 2 * count], first[2 * count :]], axis=0)
    first = jnp.concatenate(
        [first[:, :count], first[:, count : 2 * count] + first[:, 2 * count :]], axis=1
    )
    first = jnp.concatenate([first[:count], first[count:]], axis=1)

    def run(some):
        def go():
            for step in some:
                step()

        return go

    reduce_steps(
        first * scale,
        m1,
        a1,
        b1,
        c1,
        12,
        gathered,
        0,
        (run(steps[third : 2 * third]), run(steps[2 * third : 3 * third]), run(steps[3 * third :])),
    )
    basis_applied = gathered[:, :count]
    scaled_applied = gathered[:, count : 2 * count]
    basis_gram = gathered[:, 2 * count : 3 * count]
    scaled_gram = gathered[:, 3 * count :]
    row_of = lax.broadcasted_iota(jnp.int32, (count, count), 0)
    col_of = lax.broadcasted_iota(jnp.int32, (count, count), 1)
    ritz = jnp.sum(jnp.where(row_of == col_of, basis_applied, 0.0), axis=1, keepdims=True)
    correlation = basis_applied - ritz * basis_gram
    mixed = correlation + jnp.where(row_of == col_of, ritz, 0.0)
    coefficients = exact(mixed, scaled_gram) - scaled_applied
    both = stacked(jnp.concatenate([mixed, coefficients], axis=0))

    def rebuilt(block, image, scaling):
        parts = folded(dot(both, block.astype(BF16)))
        remainder = parts[:count] - image
        return scaling * remainder - parts[count:], remainder

    for t in range(each):
        value, remainder = rebuilt(base[t], applied[t], weight[t])
        seed[t] = value
        right[t] = remainder
        diag[t] = folded(dot_t(stacked(value), tiles[t]))

    landed(weight_rz, 3)
    landed(weight_rx, 4)
    landed(rz2, 7)
    landed(rx2, 8)

    def forward(slot):
        value, unused = rebuilt(rz1[slot], rz2[slot], weight_rz[slot])
        return folded(dot_t(stacked(value), tile_of(slot)))

    def backward(slot):
        there = x_of(slot)
        value, unused = rebuilt(rx1[there], rx2[there], weight_rx[there])
        return folded(dot(stacked(value), tile_of(slot)))

    return_steps(forward, (backward, prod_j2), prod_i, tx2, bz2, bx2, 9)
    landed(bz2.at[pl.ds(2, z_slots - 2)], 9)
    landed(bx2, 10)
    summed(bz2, bx2, updated)
    for t in range(each):
        updated[t] = seed[t] + weight[t] * (right[t] - (updated[t] - ritz * seed[t]))

    pack(updated, sz3, sx3)
    steps = fetch_steps(sz3, sx3, rz3, rx3, 18)
    third = (len(steps) + 3) // 4
    for step in steps[:third]:
        step()
    second = jnp.zeros((2 * count, 5 * count), F32)
    for t in range(each):
        parts = split(updated[t])
        second = second + dot_t(
            jnp.concatenate(parts, axis=0),
            jnp.concatenate([*parts, base[t].astype(BF16), *split(applied[t])], axis=0),
        )
    second = folded(second)
    second = jnp.concatenate(
        [
            second[:, :count] + second[:, count : 2 * count],
            second[:, 2 * count : 3 * count],
            second[:, 3 * count : 4 * count] + second[:, 4 * count :],
            jnp.zeros((count, count), F32),
        ],
        axis=1,
    )
    reduce_steps(
        second * scale,
        m2,
        a2,
        b2,
        c2,
        15,
        gathered,
        2,
        (run(steps[third : 2 * third]), run(steps[2 * third : 3 * third]), run(steps[3 * third :])),
    )
    new_gram = gathered[:, :count]
    overlap = gathered[:, count : 2 * count]
    new_applied = gathered[:, 2 * count : 3 * count]
    identity = (row_of == col_of).astype(F32)
    correction_gram = new_gram - exact_t(
        exact(overlap, 2.0 * identity - basis_gram), overlap
    )
    inverse = inverse_factor(correction_gram)
    turned = exact(overlap, basis_applied)
    cross = new_applied - turned
    known = exact_t(new_applied, overlap)
    known = exact_t(turned, overlap) - known - exact_t(overlap, new_applied)
    for t in range(each):
        diag[t] = updated[t] - folded(dot(stacked(overlap), base[t].astype(BF16)))
    form = jnp.zeros((2 * count, 2 * count), F32)
    for t in range(each):
        value = stacked(updated[t])
        form = form + dot_t(value, stacked(folded(dot_t(value, tiles[t]))))

    landed(rz3, 18)
    landed(rx3, 19)
    form = 0.5 * form
    for slot in range(z_slots):
        image = folded(dot_t(stacked(rz3[slot]), tile_of(slot)))
        product = dot_t(stacked(rx3[x_of(slot)]), stacked(image))
        used = z_code(slot) >= 16777216
        share = jnp.where(used, 0.5 if slot < 2 else 1.0, 0.0)
        form = form + share * product
    form = folded(form)
    form = (form[:, :count] + form[:, count:]) * scale
    lines = count // 4
    m3[...] = jnp.concatenate([form[i * lines : (i + 1) * lines] for i in range(4)], axis=1)
    spread(m3, a3, 20, "row")
    for t in range(each):
        directions[:, t * size : (t + 1) * size] = exact(inverse, diag[t])
    landed(a3, 20)
    small[...] = total(a3)
    spread(small, b3, 21, "rep")
    projected[:count, :count] = basis_applied
    projected[count:, :count] = exact(inverse, cross)
    projected[:count, count:] = exact_t(cross.T, inverse)
    landed(b3, 21)
    form = total(b3)
    form = jnp.concatenate([form[:, i * count : (i + 1) * count] for i in range(4)], axis=0)
    inner = form + form.T + known
    projected[count:, count:] = exact_t(exact(inverse, inner), inverse)

    gone(request, 0)
    for key, buffer in (
        (1, sz1),
        (2, sx1),
        (3, weight_sz),
        (4, weight_sx),
        (5, bz1.at[pl.ds(2, z_slots - 2)]),
        (6, tx1),
        (7, sz2),
        (8, sx2),
        (9, bz2.at[pl.ds(2, z_slots - 2)]),
        (10, tx2),
        (18, sz3),
        (19, sx3),
        (12, m1.at[pl.ds(0, rows - 1)]),
        (13, b1.at[pl.ds(0, reps - 1)]),
        (14, c1.at[pl.ds(0, rows - 1)]),
        (15, m2.at[pl.ds(0, rows - 1)]),
        (16, b2.at[pl.ds(0, reps - 1)]),
        (17, c2.at[pl.ds(0, rows - 1)]),
        (20, a3.at[pl.ds(0, rows - 1)]),
        (21, b3.at[pl.ds(0, reps - 1)]),
    ):
        gone(buffer, key)


def shards(basis, precond, tiles, tile_rows, tile_cols):
    count, shard = basis.shape
    size = tiles.shape[1]
    each = shard // size
    rows = lax.axis_size("row")
    reps = lax.axis_size("rep")
    chips = rows // 2
    table = request_table(tile_rows, tile_cols, each, rows, reps)
    z_slots = 2 * chips
    x_slots = 2 * (reps - 1)
    z_block = pltpu.VMEM((z_slots, count, size), F32)
    x_block = pltpu.VMEM((x_slots, count, size), F32)
    own = pltpu.VMEM((each, count, size), F32)
    part = count // rows
    lines = count // 4
    by_row = pltpu.VMEM((rows, part, 4 * count), F32)
    by_rep = pltpu.VMEM((reps, part, 4 * count), F32)
    scratch = [
        pltpu.VMEM(tiles.shape, BF16),
        pltpu.VMEM(table.shape, jnp.int32),
        pltpu.SMEM(table.shape, jnp.int32),
        own,
        pltpu.VMEM((each, 1, size), F32),
        pltpu.VMEM((z_slots, 1, size), F32),
        pltpu.VMEM((x_slots, 1, size), F32),
        pltpu.VMEM((z_slots, 1, size), F32),
        pltpu.VMEM((x_slots, 1, size), F32),
        *([z_block, x_block, z_block, x_block] * 3),
        z_block,
        z_block,
        z_block,
        x_block,
        x_block,
        z_block,
        x_block,
        z_block,
        x_block,
        *([own] * 5),
        by_row,
        by_row,
        by_rep,
        by_row,
        by_row,
        by_row,
        by_rep,
        by_row,
        pltpu.VMEM((4, part, 4 * count), F32),
        pltpu.VMEM((count, 4 * count), F32),
        pltpu.VMEM((lines, 4 * count), F32),
        pltpu.VMEM((rows, lines, 4 * count), F32),
        pltpu.VMEM((reps, lines, 4 * count), F32),
        pltpu.VMEM((lines, 4 * count), F32),
        pltpu.SemaphoreType.DMA((22,)),
        pltpu.SemaphoreType.DMA((22,)),
        pltpu.SemaphoreType.DMA((3,)),
    ]
    vmem = pl.BlockSpec(memory_space=pltpu.VMEM)
    return pl.pallas_call(
        functools.partial(kernel, rows, reps, 1.0 / (shard * rows * reps)),
        name="davidson_step",
        out_shape=(
            jax.ShapeDtypeStruct((count, shard), F32),
            jax.ShapeDtypeStruct((2 * count, 2 * count), F32),
        ),
        in_specs=[
            pl.BlockSpec(memory_space=pltpu.SMEM),
            vmem,
            vmem,
            vmem,
            pl.BlockSpec(memory_space=pl.ANY),
        ],
        out_specs=(vmem, vmem),
        scratch_shapes=scratch,
        compiler_params=pltpu.CompilerParams(
            collective_id=0, has_side_effects=True, vmem_limit_bytes=56 * 1024 * 1024
        ),
    )(table, table, basis, precond.reshape(1, shard), tiles)


def solution(mesh):
    both = ("row", "rep")
    placed = (P(None, both), P(both), P(both, None, None), P(both), P(both))
    return jax.shard_map(
        shards, mesh=mesh, in_specs=placed, out_specs=(P(None, both), P()), check_vma=False
    )
```

time: 355 us -> 147 us (0.41)
  blocking collectives: 201 us -> 0 us
  Pallas kernels: 0 us -> 140 us
  waiting for transfers between devices: 57.7 us -> 0 us
  starting transfers between devices: 30.9 us -> 0 us
  matrix products: 30.3 us -> 0 us
  other arithmetic: 17.3 us -> 2.72 us
  local copies, waits for them, and re-layouts: 15.4 us -> 3.06 us
    all_to_all x11 -> x0, blocking collectives: 201 us -> none  [the longest x7 94.9 us: from_everyone(): lax.all_to_all(jnp.broadcast_to(shard[None], (size, *shard.shape)), axis,...]
    pallas_call x0 -> x1, Pallas kernels: none -> 140 us  [shards(): pl.pallas_call(functools.partial(kernel, rows, reps, 1.0 / (shard * rows...]
    all_to_all x5 -> x0, waiting for transfers between devices: 57.7 us -> none  [the longest x1 26.8 us: apply_matrix(): lax.all_to_all(outgoing, ROW, split_axis=1, concat_axis=1, tiled=True)]
    all_to_all x5 -> x0, starting transfers between devices: 30.9 us -> none  [the longest x1 9.97 us: shards(): lax.all_to_all(requests, ROW, split_axis=0, concat_axis=0, tiled=True)]
    dot_general x24 -> x0, matrix products: 29.9 us -> none  [the longest x3 14.2 us: apply_matrix(): jnp.einsum('kjc,jrc->kjr', picked, tiles[tiles_each:], precision=highest,...]
    another operation x7 -> x0, other arithmetic: 6.78 us -> none  [the longest x3 3.6 us: shards(): factor = jnp.linalg.cholesky(correction_gram)]
    all_to_all x6 -> x0, other arithmetic: 5.23 us -> none  [the longest x4 3.89 us: from_everyone(): lax.all_to_all(jnp.broadcast_to(shard[None], (size, *shard.shape)), axis,...]
    gather x7 -> x0, local copies, waits for them, and re-layouts: 4.36 us -> none  [the longest x3 1.85 us: apply_matrix(): outgoing = jnp.take(own_blocks, wanted, axis=1)]
  transfers between devices with their start and end apart: 5 -> 0, of which waited for: 4 -> 0; matrix products, arithmetic and copies ran while one was open for 3% -> 0% of each run, Pallas kernels for 0% -> 0%
where the time goes in v1:
time: 147 us; the launch traced here: 146 us
  Pallas kernels  140 us (95%)
  local copies, waits for them, and re-layouts  3.06 us (2%)
  other arithmetic  2.72 us (2%)
    pallas_call x1, Pallas kernels, shards(): pl.pallas_call(functools.partial(kernel, rows, reps, 1.0 / (shard * rows...  140 us
    unnamed x2, local copies, waits for them, and re-layouts  3.04 us

profile of v1, /device:TPU:1, one launch (start us, length us, event | category | flops | bytes accessed | tf_op | source)
XLA Modules:
  0.0 146.3 jit_solution(4750865744282044000)
XLA Ops:
  0.7 0.7 and_select_fusion.2
  1.4 0.7 and_select_fusion.5
  2.1 0.2 convert_reduce_fusion.1
  2.3 0.2 convert_reduce_fusion
  2.5 0.2 add_reduce_fusion
  2.8 0.6 compare_select_fusion.codes.request
  3.4 139.8 %davidson_step.1 = (f32[32,2048]{1,0:T(8,128)}, f32[64,64]{1,0:T(8,128)}) custom-call(s32[23,2,128]{2,1,0:T(2,128)} %compare_select_fusion.codes.request, s32[23,2,128]{2,1,0:T(2,128)} %compare_select_fusion.codes.request, bf16[32,2048]{1,0:T(8,128)(2,1)} %basis.1, f32[1,2048]{1,0:T(1,128)} %bitcast.1, bf16[32,256,256]{2,1,0:T(8,128)(2,1)} %tiles_far.1), custom_call_target="tpu_custom_call" | custom-call | tf_op jit(solution)/shard_map/davidson_step/pallas_call | solution.py:657
  143.2 1.7 %copy.9 = f32[32,2048]{1,0:T(8,128)} copy(f32[32,2048]{1,0:T(8,128)} %get-tuple-element.14) | data formatting | bytes 524288
  144.9 1.4 copy.10
  (4 shorter events, 0.1 us)

commit v2 on v1

v2 whole, which is shorter than its diff:
```python
import functools
import math
import jax
import jax.numpy as jnp
from jax import lax
from jax.experimental import pallas as pl
from jax.experimental.pallas import tpu as pltpu
from jax.sharding import PartitionSpec as P

MESH = pl.DeviceIdType.MESH
F32 = jnp.float32
BF16 = jnp.bfloat16
HIGHEST = lax.Precision.HIGHEST


def fetches(me, peer_core, delta, chips):
    same = peer_core == me % 2
    half = chips // 2
    straight = (delta < half) | ((delta == half) & (me // 2 < half))
    return (delta == 0) | (same == straight)


def request_table(tile_rows, tile_cols, each, rows, reps):
    row = lax.axis_index("row")
    rep = lax.axis_index("rep")
    chips = rows // 2
    other_rows = tile_rows[each:]
    other_cols = tile_cols[each:]
    col_peer = other_cols // each
    row_peer = other_rows // each
    delta = lax.rem(col_peer // 2 - row // 2 + chips, chips)
    chosen = fetches(row, col_peer % 2, delta, chips)
    place = jnp.arange(other_rows.shape[0], dtype=jnp.int32)
    earlier = place[None, :] < place[:, None]
    col_rank = jnp.sum(
        (earlier & (col_peer[:, None] == col_peer[None, :])).astype(jnp.int32), axis=1
    )
    row_rank = jnp.sum(
        (earlier & chosen[None, :] & (row_peer[:, None] == row_peer[None, :])).astype(jnp.int32),
        axis=1,
    )
    z_slot = 2 * delta + col_rank
    side = math.isqrt(reps)
    shift = lax.rem(row_peer // side - rep // side + side, side) * side
    shift = shift + lax.rem(row_peer % side - rep % side + side, side)
    x_slot = 2 * (shift - 1) + row_rank
    z_code = (each + place) + x_slot * 256 + (other_cols % each) * 65536 + 16777216
    x_code = z_slot + (other_rows % each) * 65536 + 16777216
    z_slot = jnp.where(chosen, z_slot, -1)
    x_slot = jnp.where(chosen, x_slot + 2 * chips, -1)
    slots = jnp.arange(2 * (chips + reps - 1), dtype=jnp.int32)
    slots = jnp.broadcast_to(slots[:, None, None], (slots.shape[0], 128, 1))
    code = jnp.sum(
        jnp.where(slots == z_slot, z_code, 0) + jnp.where(slots == x_slot, x_code, 0), axis=2
    )
    code = jnp.where(code == 0, each * 65536, code)
    return code.reshape(chips + reps - 1, 2, 128)


def split(x):
    high = x.astype(BF16)
    low = (x - high.astype(F32)).astype(BF16)
    return high, low


def stacked(x):
    return jnp.concatenate(split(x), axis=0)


def folded(x):
    half = x.shape[0] // 2
    return x[:half] + x[half:]


def dot(a, b):
    return lax.dot_general(a, b, (((1,), (0,)), ((), ())), preferred_element_type=F32)


def dot_t(a, b):
    return lax.dot_general(a, b, (((1,), (1,)), ((), ())), preferred_element_type=F32)


def exact(a, b):
    return lax.dot_general(
        a, b, (((1,), (0,)), ((), ())), precision=HIGHEST, preferred_element_type=F32
    )


def exact_t(a, b):
    return lax.dot_general(
        a, b, (((1,), (1,)), ((), ())), precision=HIGHEST, preferred_element_type=F32
    )


def eliminated(work, begin, end):
    which = lax.broadcasted_iota(jnp.int32, (work.shape[0], 1), 0)
    for j in range(begin, end):
        scale = lax.rsqrt(work[j : j + 1, j : j + 1])
        pivot = work[j : j + 1, :] * scale
        ratio = work[:, j : j + 1] * scale
        work = jnp.where(
            which == j, pivot, work - jnp.where(which > j, ratio, 0.0) * pivot
        )
    return work


KEYS = {}
for name in ("request", "weight_z", "weight_x", "low_a", "low_b", "low_c", "mid_a", "mid_b"):
    KEYS[name] = len(KEYS)
for name in ("new_a", "new_b", "new_c", "end_a", "end_b"):
    KEYS[name] = len(KEYS)
for half in range(2):
    for name in ("z1", "x1", "bz1", "bx1", "z2", "x2", "bz2", "bx2", "z3", "x3"):
        KEYS[name, half] = len(KEYS)


def kernel(
    rows,
    reps,
    halves,
    scale,
    codes,
    request,
    basis,
    precond,
    tiles_far,
    directions,
    projected,
    tiles,
    wanted,
    wants,
    base,
    weight,
    weight_sz,
    weight_sx,
    weight_rz,
    weight_rx,
    sz1,
    sx1,
    rz1,
    rx1a,
    rx1b,
    sz2,
    sx2,
    rz2,
    rx2a,
    rx2b,
    sz3,
    sx3,
    rz3,
    rx3a,
    rx3b,
    prod_i1,
    prod_i2,
    prod_j1,
    prod_j2,
    tx1,
    tx2,
    bz1,
    bx1,
    bz2,
    bx2,
    diag,
    applied,
    right,
    seed,
    updated,
    low_m,
    low_a,
    low_b,
    low_c,
    low_piece,
    low,
    mid_m,
    mid_a,
    mid_n,
    mid_b,
    new_m,
    new_a,
    new_b,
    new_c,
    new_piece,
    new,
    end_m,
    end_a,
    end_n,
    end_b,
    send,
    recv,
    local,
):
    rx1, rx2, rx3 = (rx1a, rx1b), (rx2a, rx2b), (rx3a, rx3b)
    row = lax.axis_index("row")
    rep = lax.axis_index("rep")
    chips = rows // 2
    each = base.shape[0]
    size = base.shape[2]
    count = base.shape[1]
    z_slots = 2 * chips
    x_slots = 2 * (reps - 1)
    side = math.isqrt(reps)
    chip = row // 2
    core = lax.rem(row, 2)
    part = count // halves

    diag_load = pltpu.make_async_copy(
        tiles_far.at[pl.ds(0, each)], tiles.at[pl.ds(0, each)], local.at[0]
    )
    rest = tiles.shape[0] - each
    other_load = pltpu.make_async_copy(
        tiles_far.at[pl.ds(each, rest)], tiles.at[pl.ds(each, rest)], local.at[1]
    )
    diag_load.start()
    other_load.start()

    barrier = pltpu.get_barrier_semaphore()
    for d in range(1, rows):
        pl.semaphore_signal(
            barrier, inc=1, device_id={"row": lax.rem(row + d, rows)}, device_id_type=MESH
        )
    for d in range(1, reps):
        pl.semaphore_signal(
            barrier, inc=1, device_id={"rep": lax.rem(rep + d, reps)}, device_id_type=MESH
        )

    def z_holder(delta):
        half = chips // 2
        if delta == 0:
            other = 1 - core
        elif delta < half:
            other = core
        elif delta > half:
            other = 1 - core
        else:
            other = jnp.where(chip < half, core, 1 - core)
        return {"row": lax.rem(chip + delta, chips) * 2 + other}

    def z_reader(delta):
        half = chips // 2
        there = lax.rem(chip - delta + chips, chips)
        if delta == 0:
            other = 1 - core
        elif delta < half:
            other = core
        elif delta > half:
            other = 1 - core
        else:
            other = jnp.where(there < half, core, 1 - core)
        return {"row": there * 2 + other}

    def x_holder(sigma):
        across = lax.rem(rep // side + sigma // side, side)
        along = lax.rem(lax.rem(rep, side) + sigma % side, side)
        return {"rep": across * side + along}

    def x_reader(sigma):
        across = lax.rem(rep // side - sigma // side + side, side)
        along = lax.rem(lax.rem(rep, side) - sigma % side + side, side)
        return {"rep": across * side + along}

    def push(source, target, key, device):
        pltpu.make_async_remote_copy(
            src_ref=source,
            dst_ref=target,
            send_sem=send.at[KEYS[key]],
            recv_sem=recv.at[KEYS[key]],
            device_id=device,
            device_id_type=MESH,
        ).start()

    def landed(buffer, key):
        pltpu.make_async_copy(buffer, buffer, recv.at[KEYS[key]]).wait()

    def gone(buffer, key):
        pltpu.make_async_copy(buffer, buffer, send.at[KEYS[key]]).wait()

    def scatter(full, slots, key):
        for d in range(1, rows):
            to = lax.rem(row + d, rows)
            push(full.at[to], slots.at[row], key, {"row": to})
        pltpu.make_async_copy(full.at[row], slots.at[row], recv.at[KEYS[key]]).start()

    def spread(source, slots, key, axis):
        if axis == "row":
            me, length = row, rows
        else:
            me, length = rep, reps
        for d in range(1, length):
            push(source, slots.at[me], key, {axis: lax.rem(me + d, length)})
        pltpu.make_async_copy(source, slots.at[me], recv.at[KEYS[key]]).start()

    def total(slots):
        value = slots[0]
        for i in range(1, slots.shape[0]):
            value = value + slots[i]
        return value

    def cut(value, full):
        lines = full.shape[1]
        for i in range(full.shape[0]):
            full[i] = value[i * lines : (i + 1) * lines, :]

    def joined(slots, whole):
        lines = slots.shape[1]
        for i in range(slots.shape[0]):
            whole[i * lines : (i + 1) * lines, :] = slots[i]

    def scaled(block, scaling):
        return jnp.concatenate([block.astype(BF16), *split(block * scaling)], axis=0)

    own_low = jnp.zeros((count, 3 * count), F32)
    for t in range(each):
        block = basis[:, t * size : (t + 1) * size]
        base[t] = block.astype(F32)
        weight[t] = precond[:, t * size : (t + 1) * size]
        own_low = own_low + dot_t(block, scaled(base[t], weight[t]))
    own_low = own_low * scale
    own_low = jnp.concatenate(
        [own_low[:, :count], own_low[:, count : 2 * count] + own_low[:, 2 * count :]], axis=1
    )
    cut(jnp.concatenate([own_low[: count // 2], own_low[count // 2 :]], axis=1), low_m)

    pl.semaphore_wait(barrier, rows + reps - 2)

    for delta in range(chips):
        push(request.at[delta], wanted.at[delta], "request", z_holder(delta))
    for sigma in range(1, reps):
        here = chips + sigma - 1
        push(request.at[here], wanted.at[here], "request", x_holder(sigma))
    scatter(low_m, low_a, "low_a")

    diag_load.wait()
    for t in range(each):
        diag[t] = dot_t(basis[:, t * size : (t + 1) * size], tiles[t])

    landed(wanted, "request")
    to_scalars = pltpu.make_async_copy(wanted, wants, local.at[2])
    to_scalars.start()
    to_scalars.wait()
    landed(low_a, "low_a")
    low_piece[0] = total(low_a)
    spread(low_piece.at[0], low_b, "low_b", "rep")

    def rows_of(half):
        return slice(half * part, (half + 1) * part)

    def z_asked(slot):
        return (wants[slot // 2, slot % 2, 0] // 65536) % each

    def x_asked(slot):
        return (wants[chips + slot // 2, slot % 2, 0] // 65536) % each

    def far(size_of, index):
        return -min(index, size_of - index)

    z_order = sorted(range(chips), key=lambda delta: far(chips, delta))
    x_order = sorted(
        range(1, reps), key=lambda sigma: far(side, sigma // side) + far(side, sigma % side)
    )

    def answer(own, to_z, to_x, from_z, from_x, turn, half):
        here = rows_of(half)
        for slot in range(z_slots):
            from_z[half, slot] = own[z_asked(slot), here, :]
        for slot in range(x_slots):
            from_x[half, slot] = own[x_asked(slot), here, :]
        z_left, x_left = list(z_order), list(x_order)
        while z_left or x_left:
            for sigma in x_left[:2]:
                block = pl.ds(2 * (sigma - 1), 2)
                push(
                    from_x.at[half, block], to_x[half].at[block], ("x" + turn, half), x_reader(sigma)
                )
            for delta in z_left[:1]:
                block = pl.ds(2 * delta, 2)
                push(
                    from_z.at[half, block], to_z.at[half, block], ("z" + turn, half), z_reader(delta)
                )
            z_left, x_left = z_left[1:], x_left[2:]

    def z_code(slot):
        return codes[slot // 2, slot % 2, 0]

    def tile_of(slot):
        return tiles[z_code(slot) % 256]

    def x_of(slot):
        return (z_code(slot) // 256) % 256

    def x_source(slot):
        return codes[chips + slot // 2, slot % 2, 0] % 256

    def returned(forward, backward, images, mirrored, packed, to_z, to_x, turn, half):
        for slot in range(z_slots):
            images[half, slot] = forward(slot)
        for slot in range(x_slots):
            packed[half, slot] = images[half, x_source(slot)]
        for sigma in x_order:
            block = pl.ds(2 * (sigma - 1), 2)
            push(
                packed.at[half, block], to_x.at[half, block], ("bx" + turn, half), x_holder(sigma)
            )
        for delta in z_order[:-1]:
            for slot in (2 * delta, 2 * delta + 1):
                mirrored[half, slot] = backward(slot)
            block = pl.ds(2 * delta, 2)
            push(
                mirrored.at[half, block], to_z.at[half, block], ("bz" + turn, half), z_holder(delta)
            )

    inner = pl.ds(2, z_slots - 2)

    def summed(from_z, from_x, target, half):
        def strip(index, carry):
            here = pl.ds(pl.multiple_of(index * 8, 8), 8)
            there = pl.ds(pl.multiple_of(half * part + index * 8, 8), 8)
            totals = [diag[t, there, :] for t in range(each)]
            slots = [(from_z, slot, slot // 2, slot % 2) for slot in range(2, z_slots)]
            slots += [(from_x, slot, chips + slot // 2, slot % 2) for slot in range(x_slots)]
            for source, slot, peer, place in slots:
                value = source[half, slot, here, :]
                asked = wanted[peer, place : place + 1, :] // 65536
                for t in range(each):
                    hit = jnp.broadcast_to(asked % 256 == t, (8, 128))
                    hit = jnp.concatenate([hit] * (size // 128), axis=1)
                    totals[t] = totals[t] + jnp.where(hit, value, 0.0)
            for t in range(each):
                target[t, there, :] = totals[t]
            return carry

        lax.fori_loop(0, part // 8, strip, 0)

    def all_rows(buffer, slot):
        return jnp.concatenate([buffer[half, slot] for half in range(halves)], axis=0)

    def rows_held(buffers, slot):
        return jnp.concatenate([buffer[slot] for buffer in buffers], axis=0)

    for half in range(halves):
        answer(base, rz1, rx1, sz1, sx1, "1", half)
    for slot in range(z_slots):
        weight_sz[slot] = weight[z_asked(slot)]
    for slot in range(x_slots):
        weight_sx[slot] = weight[x_asked(slot)]
    for delta in range(chips):
        block = pl.ds(2 * delta, 2)
        push(weight_sz.at[block], weight_rz.at[block], "weight_z", z_reader(delta))
    for sigma in range(1, reps):
        block = pl.ds(2 * (sigma - 1), 2)
        push(weight_sx.at[block], weight_rx.at[block], "weight_x", x_reader(sigma))
    own_mid = jnp.zeros((2 * count, 3 * count), F32)
    for t in range(each):
        own_mid = own_mid + dot_t(stacked(diag[t]), scaled(base[t], weight[t]))
    other_load.wait()
    for half in range(halves):
        landed(rz1.at[half], ("z1", half))
        landed(rx1[half], ("x1", half))
        if half == 0:
            landed(low_b, "low_b")
            low_piece[1] = total(low_b)
            spread(low_piece.at[1], low_c, "low_c", "row")
        returned(
            lambda slot: dot_t(rz1[half, slot].astype(BF16), tile_of(slot)),
            lambda slot: dot(rx1[half][x_of(slot)].astype(BF16), tile_of(slot)),
            prod_i1,
            prod_j1,
            tx1,
            bz1,
            bx1,
            "1",
            half,
        )
    landed(low_c, "low_c")
    joined(low_c, low)
    landed(weight_rz, "weight_z")
    landed(weight_rx, "weight_x")

    def used(slot):
        return z_code(slot) >= 16777216

    own_form = own_mid[:, :count]
    both_form = jnp.zeros((2 * count, count), F32)
    scaled_form = own_mid[:, count : 2 * count] + own_mid[:, 2 * count :]
    for slot in range(z_slots):
        there = x_of(slot)
        product = dot_t(
            stacked(all_rows(prod_i1, slot)), scaled(rows_held(rx1, there), weight_rx[there])
        )
        product = jnp.where(used(slot), product, 0.0)
        if slot < 2:
            own_form = own_form + product[:, :count]
        else:
            both_form = both_form + product[:, :count]
        scaled_form = scaled_form + product[:, count : 2 * count] + product[:, 2 * count :]
        if slot >= 2:
            product = dot_t(
                stacked(all_rows(prod_j1, slot)),
                stacked(all_rows(rz1, slot) * weight_rz[slot]),
            )
            product = jnp.where(used(slot), product, 0.0)
            scaled_form = scaled_form + product[:, :count] + product[:, count:]
    both_form = folded(both_form + 0.5 * own_form)
    scaled_form = folded(scaled_form)
    quarter = jnp.concatenate([both_form, scaled_form], axis=1) * scale
    mid_m[...] = jnp.concatenate([quarter[: count // 2], quarter[count // 2 :]], axis=1)
    spread(mid_m, mid_a, "mid_a", "rep")

    for half in range(halves):
        landed(bz1.at[half, inner], ("bz1", half))
        landed(bx1.at[half], ("bx1", half))
        summed(bz1, bx1, applied, half)
        if half == halves - 1:
            landed(mid_a, "mid_a")
            mid_n[...] = total(mid_a)
            spread(mid_n, mid_b, "mid_b", "row")
        answer(applied, rz2, rx2, sz2, sx2, "2", half)
    landed(mid_b, "mid_b")
    quarter = total(mid_b)
    quarter = jnp.concatenate([quarter[:, : 2 * count], quarter[:, 2 * count :]], axis=0)
    basis_applied = quarter[:, :count] + quarter[:, :count].T
    scaled_applied = quarter[:, count:]
    basis_gram = jnp.concatenate([low[:, :count], low[:, 2 * count : 3 * count]], axis=0)
    scaled_gram = jnp.concatenate([low[:, count : 2 * count], low[:, 3 * count :]], axis=0)
    row_of = lax.broadcasted_iota(jnp.int32, (count, count), 0)
    col_of = lax.broadcasted_iota(jnp.int32, (count, count), 1)
    ritz = jnp.sum(jnp.where(row_of == col_of, basis_applied, 0.0), axis=1, keepdims=True)
    correlation = basis_applied - ritz * basis_gram
    mixed = correlation + jnp.where(row_of == col_of, ritz, 0.0)
    coefficients = exact(mixed, scaled_gram) - scaled_applied

    for half in range(halves):
        here = rows_of(half)
        both = stacked(jnp.concatenate([mixed[here], coefficients[here]], axis=0))

        def rebuilt(block, image, scaling):
            parts = folded(dot(both, block.astype(BF16)))
            remainder = parts[:part] - image
            return scaling * remainder - parts[part:], remainder

        def forward(slot):
            value, unused = rebuilt(all_rows(rz1, slot), rz2[half, slot], weight_rz[slot])
            return folded(dot_t(stacked(value), tile_of(slot)))

        def backward(slot):
            there = x_of(slot)
            value, unused = rebuilt(rows_held(rx1, there), rx2[half][there], weight_rx[there])
            return folded(dot(stacked(value), tile_of(slot)))

        landed(rz2.at[half], ("z2", half))
        landed(rx2[half], ("x2", half))
        returned(forward, backward, prod_i2, prod_j2, tx2, bz2, bx2, "2", half)
        for t in range(each):
            value, remainder = rebuilt(base[t], applied[t, here, :], weight[t])
            seed[t, here, :] = value
            right[t, here, :] = remainder
            diag[t, here, :] = folded(dot_t(stacked(value), tiles[t]))

    for half in range(halves):
        here = rows_of(half)
        landed(bz2.at[half, inner], ("bz2", half))
        landed(bx2.at[half], ("bx2", half))
        summed(bz2, bx2, updated, half)
        for t in range(each):
            value = seed[t, here, :]
            updated[t, here, :] = value + weight[t] * (
                right[t, here, :] - (updated[t, here, :] - ritz[here] * value)
            )
        if half == halves - 1:
            second = jnp.zeros((2 * count, 5 * count), F32)
            for t in range(each):
                parts = split(updated[t])
                second = second + dot_t(
                    jnp.concatenate(parts, axis=0),
                    jnp.concatenate([*parts, base[t].astype(BF16), *split(applied[t])], axis=0),
                )
            second = folded(second) * scale
            second = jnp.concatenate(
                [
                    second[:, :count] + second[:, count : 2 * count],
                    second[:, 2 * count : 3 * count],
                    second[:, 3 * count : 4 * count] + second[:, 4 * count :],
                    jnp.zeros((count, count), F32),
                ],
                axis=1,
            )
            cut(second, new_m)
            scatter(new_m, new_a, "new_a")
        answer(updated, rz3, rx3, sz3, sx3, "3", half)
    form = jnp.zeros((2 * count, 2 * count), F32)
    for t in range(each):
        value = stacked(updated[t])
        form = form + dot_t(value, stacked(folded(dot_t(value, tiles[t]))))
    form = 0.5 * form
    landed(new_a, "new_a")
    new_piece[0] = total(new_a)
    spread(new_piece.at[0], new_b, "new_b", "rep")
    for half in range(halves):
        landed(rz3.at[half], ("z3", half))
        landed(rx3[half], ("x3", half))
        if half == halves - 1:
            landed(new_b, "new_b")
            new_piece[1] = total(new_b)
            spread(new_piece.at[1], new_c, "new_c", "row")
        for slot in range(z_slots):
            prod_i2[half, slot] = folded(dot_t(stacked(rz3[half, slot]), tile_of(slot)))
    for slot in range(z_slots):
        product = dot_t(stacked(rows_held(rx3, x_of(slot))), stacked(all_rows(prod_i2, slot)))
        form = form + jnp.where(used(slot), 0.5 if slot < 2 else 1.0, 0.0) * product
    form = folded(form)
    form = (form[:, :count] + form[:, count:]) * scale
    lines = count // 4
    end_m[...] = jnp.concatenate([form[i * lines : (i + 1) * lines] for i in range(4)], axis=1)
    spread(end_m, end_a, "end_a", "row")

    landed(new_c, "new_c")
    joined(new_c, new)
    new_gram = new[:, :count]
    overlap = new[:, count : 2 * count]
    new_applied = new[:, 2 * count : 3 * count]
    identity = (row_of == col_of).astype(F32)
    correction_gram = new_gram - exact_t(exact(overlap, 2.0 * identity - basis_gram), overlap)
    work = eliminated(jnp.concatenate([correction_gram, identity], axis=1), 0, count // 2)
    landed(end_a, "end_a")
    end_n[...] = total(end_a)
    spread(end_n, end_b, "end_b", "rep")
    inverse = eliminated(work, count // 2, count)[:, count:]
    turned = exact(overlap, basis_applied)
    cross = new_applied - turned
    known = exact_t(new_applied, overlap)
    known = exact_t(turned, overlap) - known - exact_t(overlap, new_applied)
    projected[:count, :count] = basis_applied
    projected[count:, :count] = exact(inverse, cross)
    projected[:count, count:] = exact_t(cross.T, inverse)
    for t in range(each):
        value = updated[t] - folded(dot(stacked(overlap), base[t].astype(BF16)))
        directions[:, t * size : (t + 1) * size] = exact(inverse, value)
    landed(end_b, "end_b")
    form = total(end_b)
    form = jnp.concatenate([form[:, i * count : (i + 1) * count] for i in range(4)], axis=0)
    middle = form + form.T + known
    projected[count:, count:] = exact_t(exact(inverse, middle), inverse)

    gone(request, "request")
    gone(weight_sz, "weight_z")
    gone(weight_sx, "weight_x")
    for half in range(halves):
        for turn, from_z, from_x in (("1", sz1, sx1), ("2", sz2, sx2), ("3", sz3, sx3)):
            gone(from_z.at[half], ("z" + turn, half))
            gone(from_x.at[half], ("x" + turn, half))
        for turn, from_z, from_x in (("1", prod_j1, tx1), ("2", prod_j2, tx2)):
            gone(from_z.at[half, inner], ("bz" + turn, half))
            gone(from_x.at[half], ("bx" + turn, half))
    other_rows = pl.ds(0, rows - 1)
    other_reps = pl.ds(0, reps - 1)
    for key, buffer in (
        ("low_a", low_a.at[other_rows]),
        ("low_b", low_b.at[other_reps]),
        ("low_c", low_c.at[other_rows]),
        ("mid_a", mid_a.at[other_reps]),
        ("mid_b", mid_b.at[other_rows]),
        ("new_a", new_a.at[other_rows]),
        ("new_b", new_b.at[other_reps]),
        ("new_c", new_c.at[other_rows]),
        ("end_a", end_a.at[other_rows]),
        ("end_b", end_b.at[other_reps]),
    ):
        gone(buffer, key)


def shards(basis, precond, tiles, tile_rows, tile_cols):
    count, shard = basis.shape
    size = tiles.shape[1]
    each = shard // size
    rows = lax.axis_size("row")
    reps = lax.axis_size("rep")
    chips = rows // 2
    halves = 2
    table = request_table(tile_rows, tile_cols, each, rows, reps)
    z_slots = 2 * chips
    x_slots = 2 * (reps - 1)

    def held(*shape):
        return pltpu.VMEM(shape, F32)

    z_block = held(halves, z_slots, count // halves, size)
    x_block = held(halves, x_slots, count // halves, size)
    x_half = held(x_slots, count // halves, size)
    own = held(each, count, size)
    wide = 4 * count
    lines = count // rows
    scratch = [
        pltpu.VMEM(tiles.shape, BF16),
        pltpu.VMEM(table.shape, jnp.int32),
        pltpu.SMEM(table.shape, jnp.int32),
        own,
        held(each, 1, size),
        held(z_slots, 1, size),
        held(x_slots, 1, size),
        held(z_slots, 1, size),
        held(x_slots, 1, size),
        *([z_block, x_block, z_block, *([x_half] * halves)] * 3),
        z_block,
        z_block,
        z_block,
        z_block,
        x_block,
        x_block,
        z_block,
        x_block,
        z_block,
        x_block,
        *([own] * 5),
        held(rows, lines // 2, wide),
        held(rows, lines // 2, wide),
        held(reps, lines // 2, wide),
        held(rows, lines // 2, wide),
        held(2, lines // 2, wide),
        held(count // 2, wide),
        held(count // 2, wide),
        held(reps, count // 2, wide),
        held(count // 2, wide),
        held(rows, count // 2, wide),
        held(rows, lines, wide),
        held(rows, lines, wide),
        held(reps, lines, wide),
        held(rows, lines, wide),
        held(2, lines, wide),
        held(count, wide),
        held(count // 4, wide),
        held(rows, count // 4, wide),
        held(count // 4, wide),
        held(reps, count // 4, wide),
        pltpu.SemaphoreType.DMA((len(KEYS),)),
        pltpu.SemaphoreType.DMA((len(KEYS),)),
        pltpu.SemaphoreType.DMA((3,)),
    ]
    vmem = pl.BlockSpec(memory_space=pltpu.VMEM)
    return pl.pallas_call(
        functools.partial(kernel, rows, reps, halves, 1.0 / (shard * rows * reps)),
        name="davidson_step",
        out_shape=(
            jax.ShapeDtypeStruct((count, shard), F32),
            jax.ShapeDtypeStruct((2 * count, 2 * count), F32),
        ),
        in_specs=[
            pl.BlockSpec(memory_space=pltpu.SMEM),
            vmem,
            vmem,
            vmem,
            pl.BlockSpec(memory_space=pl.ANY),
        ],
        out_specs=(vmem, vmem),
        scratch_shapes=scratch,
        compiler_params=pltpu.CompilerParams(
            collective_id=0, has_side_effects=True, vmem_limit_bytes=56 * 1024 * 1024
        ),
    )(table, table, basis, precond.reshape(1, shard), tiles)


def solution(mesh):
    both = ("row", "rep")
    placed = (P(None, both), P(both), P(both, None, None), P(both), P(both))
    return jax.shard_map(
        shards, mesh=mesh, in_specs=placed, out_specs=(P(None, both), P()), check_vma=False
    )
```

time: 147 us -> 106 us (0.72)
  Pallas kernels: 140 us -> 99.4 us
    pallas_call x1, Pallas kernels: 140 us -> 99.4 us  [shards(): pl.pallas_call(functools.partial(kernel, rows, reps, halves, 1.0 / (shard...]
where the time goes in v2:
time: 106 us
  Pallas kernels  99.4 us (94%)
  local copies, waits for them, and re-layouts  3.06 us (3%)
  other arithmetic  2.73 us (3%)
    pallas_call x1, Pallas kernels, shards(): pl.pallas_call(functools.partial(kernel, rows, reps, halves, 1.0 / (shard...  99.4 us
    unnamed x2, local copies, waits for them, and re-layouts  3.04 us

profile of v2, /device:TPU:1, one launch (start us, length us, event | category | flops | bytes accessed | tf_op | source)
XLA Modules:
  0.0 105.9 jit_solution(16403283284492802628)
XLA Ops:
  0.7 0.7 and_select_fusion.4
  1.4 0.7 and_select_fusion.7
  2.1 0.2 convert_reduce_fusion.1
  2.4 0.2 convert_reduce_fusion
  2.6 0.2 add_reduce_fusion
  2.8 0.6 compare_select_fusion.codes.request
  3.4 99.4 %davidson_step.1 = (f32[32,2048]{1,0:T(8,128)}, f32[64,64]{1,0:T(8,128)}) custom-call(s32[23,2,128]{2,1,0:T(2,128)} %compare_select_fusion.codes.request, s32[23,2,128]{2,1,0:T(2,128)} %compare_select_fusion.codes.request, bf16[32,2048]{1,0:T(8,128)(2,1)} %basis.1, f32[1,2048]{1,0:T(1,128)} %bitcast.1, bf16[32,256,256]{2,1,0:T(8,128)(2,1)} %tiles_far.1), custom_call_target="tpu_custom_call" | custom-call | tf_op jit(solution)/shard_map/davidson_step/pallas_call | solution.py:738
  102.9 1.7 %copy.9 = f32[32,2048]{1,0:T(8,128)} copy(f32[32,2048]{1,0:T(8,128)} %get-tuple-element.14) | data formatting | bytes 524288
  104.6 1.4 %copy.10 = f32[64,64]{1,0:T(8,128)} copy(f32[64,64]{1,0:T(8,128)} %get-tuple-element.15) | data formatting | bytes 32768
  (4 shorter events, 0.1 us)

commit v3 on v2

--- a/solution.py
+++ b/solution.py
@@ -13,48 +13,43 @@
 HIGHEST = lax.Precision.HIGHEST
 
 
-def fetches(me, peer_core, delta, chips):
-    same = peer_core == me % 2
-    half = chips // 2
-    straight = (delta < half) | ((delta == half) & (me // 2 < half))
-    return (delta == 0) | (same == straight)
-
-
-def request_table(tile_rows, tile_cols, each, rows, reps):
-    row = lax.axis_index("row")
-    rep = lax.axis_index("rep")
+def request_table(tile_rows, tile_cols, row, rep, each, rows, reps):
+    entries = tile_rows.shape[1]
     chips = rows // 2
-    other_rows = tile_rows[each:]
-    other_cols = tile_cols[each:]
-    col_peer = other_cols // each
-    row_peer = other_rows // each
-    delta = lax.rem(col_peer // 2 - row // 2 + chips, chips)
-    chosen = fetches(row, col_peer % 2, delta, chips)
-    place = jnp.arange(other_rows.shape[0], dtype=jnp.int32)
-    earlier = place[None, :] < place[:, None]
-    col_rank = jnp.sum(
-        (earlier & (col_peer[:, None] == col_peer[None, :])).astype(jnp.int32), axis=1
-    )
-    row_rank = jnp.sum(
-        (earlier & chosen[None, :] & (row_peer[:, None] == row_peer[None, :])).astype(jnp.int32),
-        axis=1,
-    )
-    z_slot = 2 * delta + col_rank
     side = math.isqrt(reps)
-    shift = lax.rem(row_peer // side - rep // side + side, side) * side
-    shift = shift + lax.rem(row_peer % side - rep % side + side, side)
-    x_slot = 2 * (shift - 1) + row_rank
-    z_code = (each + place) + x_slot * 256 + (other_cols % each) * 65536 + 16777216
-    x_code = z_slot + (other_rows % each) * 65536 + 16777216
+    bits = each.bit_length() - 1
+    side_bits = side.bit_length() - 1
+    place = lax.broadcasted_iota(jnp.int32, (1, entries), 1)
+    col_peer = lax.shift_right_logical(tile_cols, bits)
+    row_peer = lax.shift_right_logical(tile_rows, bits)
+    delta = (lax.shift_right_logical(col_peer, 1) - row // 2 + chips) & (chips - 1)
+    limit = chips // 2 + jnp.where(row // 2 < chips // 2, 1, 0)
+    differs = (col_peer & 1) ^ lax.rem(row, 2)
+    crossed = jnp.where(delta < limit, 0, 1)
+    chosen = ((delta == 0) | (differs == crossed)) & (place >= each)
+    col_key = jnp.where(chosen, col_peer, -1)
+    row_key = jnp.where(chosen, row_peer, -1)
+    first = lax.broadcasted_iota(jnp.int32, (entries, entries), 0)
+    second = lax.broadcasted_iota(jnp.int32, (entries, entries), 1)
+
+    def rank(key):
+        upright = jnp.sum(jnp.where(first == second, key, 0), axis=1, keepdims=True)
+        return jnp.sum(
+            jnp.where((first < second) & (upright == key), 1, 0), axis=0, keepdims=True
+        )
+
+    across = (lax.shift_right_logical(row_peer, side_bits) - rep // side + side) & (side - 1)
+    along = ((row_peer & (side - 1)) - lax.rem(rep, side) + side) & (side - 1)
+    z_slot = 2 * delta + rank(col_key)
+    x_slot = 2 * (across * side + along - 1) + rank(row_key)
+    z_code = place + x_slot * 256 + (tile_cols & (each - 1)) * 65536 + 16777216
+    x_code = z_slot + (tile_rows & (each - 1)) * 65536 + 16777216
     z_slot = jnp.where(chosen, z_slot, -1)
     x_slot = jnp.where(chosen, x_slot + 2 * chips, -1)
-    slots = jnp.arange(2 * (chips + reps - 1), dtype=jnp.int32)
-    slots = jnp.broadcast_to(slots[:, None, None], (slots.shape[0], 128, 1))
-    code = jnp.sum(
-        jnp.where(slots == z_slot, z_code, 0) + jnp.where(slots == x_slot, x_code, 0), axis=2
-    )
-    code = jnp.where(code == 0, each * 65536, code)
-    return code.reshape(chips + reps - 1, 2, 128)
+    slots = lax.broadcasted_iota(jnp.int32, (2 * (chips + reps), entries), 0)
+    code = jnp.where(slots == z_slot, z_code, 0) + jnp.where(slots == x_slot, x_code, 0)
+    code = jnp.sum(code, axis=1, keepdims=True)
+    return jnp.broadcast_to(jnp.where(code == 0, each * 65536, code), (code.shape[0], 128))
 
 
 def split(x):
@@ -119,13 +114,17 @@
     reps,
     halves,
     scale,
-    codes,
-    request,
-    basis,
-    precond,
+    tile_rows,
+    tile_cols,
+    basis_far,
+    precond_far,
     tiles_far,
     directions,
     projected,
+    request,
+    codes,
+    basis,
+    precond,
     tiles,
     wanted,
     wants,
@@ -203,6 +202,20 @@
     core = lax.rem(row, 2)
     part = count // halves
 
+    barrier = pltpu.get_barrier_semaphore()
+    for d in range(1, rows):
+        pl.semaphore_signal(
+            barrier, inc=1, device_id={"row": lax.rem(row + d, rows)}, device_id_type=MESH
+        )
+    for d in range(1, reps):
+        pl.semaphore_signal(
+            barrier, inc=1, device_id={"rep": lax.rem(rep + d, reps)}, device_id_type=MESH
+        )
+
+    basis_load = pltpu.make_async_copy(basis_far, basis, local.at[3])
+    precond_load = pltpu.make_async_copy(precond_far, precond, local.at[4])
+    basis_load.start()
+    precond_load.start()
     diag_load = pltpu.make_async_copy(
         tiles_far.at[pl.ds(0, each)], tiles.at[pl.ds(0, each)], local.at[0]
     )
@@ -212,16 +225,6 @@
     )
     diag_load.start()
     other_load.start()
-
-    barrier = pltpu.get_barrier_semaphore()
-    for d in range(1, rows):
-        pl.semaphore_signal(
-            barrier, inc=1, device_id={"row": lax.rem(row + d, rows)}, device_id_type=MESH
-        )
-    for d in range(1, reps):
-        pl.semaphore_signal(
-            barrier, inc=1, device_id={"rep": lax.rem(rep + d, reps)}, device_id_type=MESH
-        )
 
     def z_holder(delta):
         half = chips // 2
@@ -308,6 +311,11 @@
     def scaled(block, scaling):
         return jnp.concatenate([block.astype(BF16), *split(block * scaling)], axis=0)
 
+    table = request_table(tile_rows[...], tile_cols[...], row, rep, each, rows, reps)
+    for peer in range(request.shape[0]):
+        request[peer] = table[2 * peer : 2 * peer + 2]
+    basis_load.wait()
+    precond_load.wait()
     own_low = jnp.zeros((count, 3 * count), F32)
     for t in range(each):
         block = basis[:, t * size : (t + 1) * size]
@@ -328,6 +336,8 @@
         here = chips + sigma - 1
         push(request.at[here], wanted.at[here], "request", x_holder(sigma))
     scatter(low_m, low_a, "low_a")
+    code_load = pltpu.make_async_copy(request, codes, local.at[5])
+    code_load.start()
 
     diag_load.wait()
     for t in range(each):
@@ -337,6 +347,7 @@
     to_scalars = pltpu.make_async_copy(wanted, wants, local.at[2])
     to_scalars.start()
     to_scalars.wait()
+    code_load.wait()
     landed(low_a, "low_a")
     low_piece[0] = total(low_a)
     spread(low_piece.at[0], low_b, "low_b", "rep")
@@ -345,10 +356,10 @@
         return slice(half * part, (half + 1) * part)
 
     def z_asked(slot):
-        return (wants[slot // 2, slot % 2, 0] // 65536) % each
+        return lax.shift_right_logical(wants[slot // 2, slot % 2, 0], 16) & (each - 1)
 
     def x_asked(slot):
-        return (wants[chips + slot // 2, slot % 2, 0] // 65536) % each
+        return lax.shift_right_logical(wants[chips + slot // 2, slot % 2, 0], 16) & (each - 1)
 
     def far(size_of, index):
         return -min(index, size_of - index)
@@ -382,13 +393,13 @@
         return codes[slot // 2, slot % 2, 0]
 
     def tile_of(slot):
-        return tiles[z_code(slot) % 256]
+        return tiles[jnp.minimum(z_code(slot) & 255, tiles.shape[0] - 1)]
 
     def x_of(slot):
-        return (z_code(slot) // 256) % 256
+        return jnp.minimum(lax.shift_right_logical(z_code(slot), 8) & 255, x_slots - 1)
 
     def x_source(slot):
-        return codes[chips + slot // 2, slot % 2, 0] % 256
+        return jnp.minimum(codes[chips + slot // 2, slot % 2, 0] & 255, z_slots - 1)
 
     def returned(forward, backward, images, mirrored, packed, to_z, to_x, turn, half):
         for slot in range(z_slots):
@@ -419,9 +430,9 @@
             slots += [(from_x, slot, chips + slot // 2, slot % 2) for slot in range(x_slots)]
             for source, slot, peer, place in slots:
                 value = source[half, slot, here, :]
-                asked = wanted[peer, place : place + 1, :] // 65536
+                asked = lax.shift_right_logical(wanted[peer, place : place + 1, :], 16) & 255
                 for t in range(each):
-                    hit = jnp.broadcast_to(asked % 256 == t, (8, 128))
+                    hit = jnp.broadcast_to(asked == t, (8, 128))
                     hit = jnp.concatenate([hit] * (size // 128), axis=1)
                     totals[t] = totals[t] + jnp.where(hit, value, 0.0)
             for t in range(each):
@@ -667,6 +678,11 @@
         gone(buffer, key)
 
 
+def publish(directions, projected, directions_out, projected_out):
+    directions_out[...] = directions[...]
+    projected_out[...] = projected[...]
+
+
 def shards(basis, precond, tiles, tile_rows, tile_cols):
     count, shard = basis.shape
     size = tiles.shape[1]
@@ -675,7 +691,7 @@
     reps = lax.axis_size("rep")
     chips = rows // 2
     halves = 2
-    table = request_table(tile_rows, tile_cols, each, rows, reps)
+    asked = (chips + reps - 1, 2, 128)
     z_slots = 2 * chips
     x_slots = 2 * (reps - 1)
 
@@ -689,9 +705,13 @@
     wide = 4 * count
     lines = count // rows
     scratch = [
+        pltpu.VMEM(asked, jnp.int32),
+        pltpu.SMEM(asked, jnp.int32),
+        pltpu.VMEM(basis.shape, BF16),
+        held(1, shard),
         pltpu.VMEM(tiles.shape, BF16),
-        pltpu.VMEM(table.shape, jnp.int32),
-        pltpu.SMEM(table.shape, jnp.int32),
+        pltpu.VMEM(asked, jnp.int32),
+        pltpu.SMEM(asked, jnp.int32),
         own,
         held(each, 1, size),
         held(z_slots, 1, size),
@@ -732,29 +752,37 @@
         held(reps, count // 4, wide),
         pltpu.SemaphoreType.DMA((len(KEYS),)),
         pltpu.SemaphoreType.DMA((len(KEYS),)),
-        pltpu.SemaphoreType.DMA((3,)),
+        pltpu.SemaphoreType.DMA((6,)),
     ]
     vmem = pl.BlockSpec(memory_space=pltpu.VMEM)
-    return pl.pallas_call(
+    far_away = pl.BlockSpec(memory_space=pl.ANY)
+    found = pl.pallas_call(
         functools.partial(kernel, rows, reps, halves, 1.0 / (shard * rows * reps)),
         name="davidson_step",
         out_shape=(
             jax.ShapeDtypeStruct((count, shard), F32),
             jax.ShapeDtypeStruct((2 * count, 2 * count), F32),
         ),
-        in_specs=[
-            pl.BlockSpec(memory_space=pltpu.SMEM),
-            vmem,
-            vmem,
-            vmem,
-            pl.BlockSpec(memory_space=pl.ANY),
-        ],
+        in_specs=[vmem, vmem, far_away, far_away, far_away],
         out_specs=(vmem, vmem),
         scratch_shapes=scratch,
         compiler_params=pltpu.CompilerParams(
-            collective_id=0, has_side_effects=True, vmem_limit_bytes=56 * 1024 * 1024
+            collective_id=0, has_side_effects=True, vmem_limit_bytes=60 * 1024 * 1024
         ),
-    )(table, table, basis, precond.reshape(1, shard), tiles)
+    )(
+        tile_rows.reshape(1, tile_rows.shape[0]),
+        tile_cols.reshape(1, tile_cols.shape[0]),
+        basis,
+        precond.reshape(1, shard),
+        tiles,
+    )
+    return pl.pallas_call(
+        publish,
+        name="publish",
+        out_shape=tuple(jax.ShapeDtypeStruct(a.shape, a.dtype) for a in found),
+        in_specs=[vmem, vmem],
+        out_specs=(vmem, vmem),
+    )(*found)
 
 
 def solution(mesh):

time: 106 us -> 100 us (0.943)
  local copies, waits for them, and re-layouts: 3.06 us -> 0 us
  other arithmetic: 2.73 us -> 0 us
    unnamed x2 -> x0, local copies, waits for them, and re-layouts: 3.04 us -> none
    select_n x5 -> x0, other arithmetic: 2.12 us -> none  [the longest x1 0.73 us: request_table(): row_peer = other_rows // each]
    pallas_call x0 -> x1, Pallas kernels: none -> 1.68 us  [shards(): pl.pallas_call(publish, name='publish', out_shape=tuple((jax.ShapeDtypeSt...]
    pallas_call x1, Pallas kernels: 99.4 us -> 97.9 us  [shards(): pl.pallas_call(functools.partial(kernel, rows, reps, halves, 1.0 / (shard...]
where the time goes in v3:
time: 100 us
  Pallas kernels  99.6 us (100%)
    pallas_call x1, Pallas kernels, shards(): pl.pallas_call(functools.partial(kernel, rows, reps, halves, 1.0 / (shard...  97.9 us

profile of v3, /device:TPU:1, one launch (start us, length us, event | category | flops | bytes accessed | tf_op | source)
XLA Modules:
  0.0 100.2 jit_solution(2632045477113346683)
XLA Ops:
  0.6 97.9 %davidson_step.1 = (f32[32,2048]{1,0:T(8,128)}, f32[64,64]{1,0:T(8,128)}) custom-call(s32[1,32]{1,0:T(1,128)} %bitcast.4, s32[1,32]{1,0:T(1,128)} %bitcast.5, bf16[32,2048]{1,0:T(8,128)(2,1)} %basis_far.1, f32[1,2048]{1,0:T(1,128)} %bitcast.3, bf16[32,256,256]{2,1,0:T(8,128)(2,1)} %tiles_far.1), custom_call_target="tpu_custom_call" | custom-call | tf_op jit(solution)/shard_map/davidson_step/pallas_call | solution.py:759
  98.5 1.7 %publish.1 = (f32[32,2048]{1,0:T(8,128)}, f32[64,64]{1,0:T(8,128)}) custom-call(f32[32,2048]{1,0:T(8,128)} %get-tuple-element.4.directions, f32[64,64]{1,0:T(8,128)} %get-tuple-element.5.projected), custom_call_target="tpu_custom_call" | custom-call | tf_op jit(solution)/shard_map/publish/pallas_call | solution.py:779

commit v4 on v3

--- a/solution.py
+++ b/solution.py
@@ -514,7 +514,7 @@
     scaled_form = folded(scaled_form)
     quarter = jnp.concatenate([both_form, scaled_form], axis=1) * scale
     mid_m[...] = jnp.concatenate([quarter[: count // 2], quarter[count // 2 :]], axis=1)
-    spread(mid_m, mid_a, "mid_a", "rep")
+    spread(mid_m, mid_a, "mid_a", "row")
 
     for half in range(halves):
         landed(bz1.at[half, inner], ("bz1", half))
@@ -523,7 +523,7 @@
         if half == halves - 1:
             landed(mid_a, "mid_a")
             mid_n[...] = total(mid_a)
-            spread(mid_n, mid_b, "mid_b", "row")
+            spread(mid_n, mid_b, "mid_b", "rep")
         answer(applied, rz2, rx2, sz2, sx2, "2", half)
     landed(mid_b, "mid_b")
     quarter = total(mid_b)
@@ -667,8 +667,8 @@
         ("low_a", low_a.at[other_rows]),
         ("low_b", low_b.at[other_reps]),
         ("low_c", low_c.at[other_rows]),
-        ("mid_a", mid_a.at[other_reps]),
-        ("mid_b", mid_b.at[other_rows]),
+        ("mid_a", mid_a.at[other_rows]),
+        ("mid_b", mid_b.at[other_reps]),
         ("new_a", new_a.at[other_rows]),
         ("new_b", new_b.at[other_reps]),
         ("new_c", new_c.at[other_rows]),
@@ -737,9 +737,9 @@
         held(2, lines // 2, wide),
         held(count // 2, wide),
         held(count // 2, wide),
+        held(rows, count // 2, wide),
+        held(count // 2, wide),
         held(reps, count // 2, wide),
-        held(count // 2, wide),
-        held(rows, count // 2, wide),
         held(rows, lines, wide),
         held(rows, lines, wide),
         held(reps, lines, wide),

time: 100 us -> 102 us (1.020)
  Pallas kernels: 99.6 us -> 101 us
    pallas_call x1, Pallas kernels: 97.9 us -> 99.3 us  [shards(): pl.pallas_call(functools.partial(kernel, rows, reps, halves, 1.0 / (shard...]
where the time goes in v4:
time: 102 us
  Pallas kernels  101 us (99%)
    pallas_call x1, Pallas kernels, shards(): pl.pallas_call(functools.partial(kernel, rows, reps, halves, 1.0 / (shard...  99.3 us

profile of v4, /device:TPU:1, one launch (start us, length us, event | category | flops | bytes accessed | tf_op | source)
XLA Modules:
  0.0 101.6 jit_solution(6334608071662399634)
XLA Ops:
  0.6 99.3 %davidson_step.1 = (f32[32,2048]{1,0:T(8,128)}, f32[64,64]{1,0:T(8,128)}) custom-call(s32[1,32]{1,0:T(1,128)} %bitcast.4, s32[1,32]{1,0:T(1,128)} %bitcast.5, bf16[32,2048]{1,0:T(8,128)(2,1)} %basis_far.1, f32[1,2048]{1,0:T(1,128)} %bitcast.3, bf16[32,256,256]{2,1,0:T(8,128)(2,1)} %tiles_far.1), custom_call_target="tpu_custom_call" | custom-call | tf_op jit(solution)/shard_map/davidson_step/pallas_call | solution.py:759
  99.9 1.7 %publish.1 = (f32[32,2048]{1,0:T(8,128)}, f32[64,64]{1,0:T(8,128)}) custom-call(f32[32,2048]{1,0:T(8,128)} %get-tuple-element.4.directions, f32[64,64]{1,0:T(8,128)} %get-tuple-element.5.projected), custom_call_target="tpu_custom_call" | custom-call | tf_op jit(solution)/shard_map/publish/pallas_call | solution.py:779
